TPU v7x, 256 devices: a whole 4x4x8 slice. The times are simulated.
256 devices in a mesh: lat: 8 (over x, core), lon: 32 (over y, z).
Axes of the slice: x: 4, y: 4, z: 8, core: 2. Of those that a mesh axis runs over, the one named last changes fastest.
Arguments:
- velocity: bfloat16 [2, 256, 1536, 1024], P(None, None, 'lon', 'lat'), may hold values from -16 to 16
- lon_metric: float32 [1536, 1024], P('lon', 'lat'), may hold values from 0.5 to 2
- lat_metric: float32 [1536, 1024], P('lon', 'lat'), may hold values from 0.5 to 2
- wet_index: int32 [1572864], P(('lat', 'lon')), may hold values from 0 to 6143, as said below
- wet_count: int32 [256], P(('lat', 'lon')), may hold values from 3072 to 6144, as said below
Outputs:
- basis: bfloat16 [512, 1572864], P(None, ('lat', 'lon'))
- r_factor: float32 [512, 512], replicated
Inputs may be any that keep to these rules, and one draw needn't show every extreme that they name: `wet_index`: each device's 6144 entries are a permutation of its local cells 0 to 6143. `wet_count`: some device has all 6144 cells wet.
All inputs are finite; a program needn't handle non-finite values.
Results may differ from a plain program's by a relative error of at most 0.001.
The roundings to bfloat16 on the way count: a program that leaves them out, or rounds other values in their place, can miss the bound.
Values may be sent and summed in bfloat16 or wider, within the bound.
A program may use at most 128 MiB of HBM per device.

v0:
```python
import math

import jax
import jax.numpy as jnp
from jax import lax
from jax.sharding import Mesh
from jax.sharding import PartitionSpec as P

LON = ("lon_0", "lon_1")
LAT = ("lat_0", "lat_1")
LAT_LON = ("lat_0", "lat_1", "lon_0", "lon_1")


def with_halo(block, sides, width, periodic):
    for axis, dim in sides:
        count = lax.axis_size(axis)
        forward = [(i, i + 1) for i in range(count - 1)]
        if periodic:
            forward.append((count - 1, 0))
        backward = [(target, source) for source, target in forward]
        low = lax.ppermute(
            lax.slice_in_dim(block, block.shape[dim] - width, None, axis=dim), axis, forward
        )
        high = lax.ppermute(lax.slice_in_dim(block, 0, width, axis=dim), axis, backward)
        block = jnp.concatenate([low, block, high], axis=dim)
    return block


def partner(block, axis, stride):
    count = lax.axis_size(axis)
    route = []
    for low in range(count):
        high = low | 1 << stride
        if high != low and high < count:
            route += [(low, high), (high, low)]
    return lax.ppermute(block, axis, route)


def in_blocks(value, dim, size):
    before, after = (value.shape[:dim], value.shape[dim + 1 :])
    return jnp.moveaxis(value.reshape(*before, size, -1, *after), dim, 0)


def sent_and_summed(value, axis, dim):
    parts = in_blocks(value, dim, lax.axis_size(axis))
    arrived = lax.all_to_all(parts, axis, split_axis=0, concat_axis=0, tiled=True)
    return arrived.sum(axis=0)


def sum_by_axis(value, axes, dim):
    far, near = axes
    parts = in_blocks(value, dim, lax.axis_size(far))
    nearer = sent_and_summed(parts, near, dim + 1)
    arrived = lax.all_to_all(nearer, far, split_axis=0, concat_axis=0, tiled=True)
    return arrived.sum(axis=0)


def rows_for(lines, size):
    spare = -lines.shape[0] % size
    if not spare:
        return lines
    return jnp.concatenate([lines, jnp.zeros((spare, *lines.shape[1:]), lines.dtype)])


def from_everyone(value, axis):
    size = lax.axis_size(axis)
    return lax.all_to_all(
        jnp.broadcast_to(value[None], (size, *value.shape)), axis, 0, 0, tiled=True
    )


def in_order(parts, dim):
    shape = list(parts.shape[1:])
    shape[dim] *= parts.shape[0]
    return jnp.moveaxis(parts, 0, dim).reshape(shape)


def gather_axes(value, axes, dim):
    far, near = axes
    parts = from_everyone(from_everyone(value, far), near)
    return in_order(parts.swapaxes(0, 1).reshape(-1, *value.shape), dim)


def sum_by_parts(value, axes):
    lines = value.reshape(-1, value.shape[-1])
    own = sum_by_axis(rows_for(lines, lax.axis_size(axes[0]) * lax.axis_size(axes[1])), axes, 0)
    whole = gather_axes(own, axes, 0)
    return whole[: len(lines)].reshape(value.shape)


def upper_blocks(gram, block_size):
    block_count = gram.shape[0] // block_size
    return jnp.stack(
        [
            gram[
                row_at * block_size : (row_at + 1) * block_size,
                col_at * block_size : (col_at + 1) * block_size,
            ]
            for row_at in range(block_count)
            for col_at in range(row_at, block_count)
        ]
    )


def from_blocks(pieces, block_count):
    places = {}
    position = 0
    for row_at in range(block_count):
        for col_at in range(row_at, block_count):
            places[row_at, col_at] = pieces[position]
            position += 1
    return jnp.block(
        [
            [
                places[row_at, col_at] if col_at >= row_at else places[col_at, row_at].T
                for col_at in range(block_count)
            ]
            for row_at in range(block_count)
        ]
    )


def shards(velocity, lon_metric, lat_metric, wet_index, wet_count):
    days = velocity.shape[1]
    width_x = velocity.shape[2]
    width_y = velocity.shape[3]
    cells = width_x * width_y
    columns = 2 * days
    lon_ext = with_halo(velocity, ((LON, 2),), 1, True)
    lat_ext = with_halo(velocity, ((LAT, 3),), 1, False)
    mirrored = velocity[:, :, ::-1, -1].reshape(-1)
    bit_count = lax.axis_size(LON).bit_length() - 1
    for bit_pos in range(bit_count):
        mirrored = partner(mirrored, LON, bit_pos)
    ghost_row = -mirrored.reshape(2, days, width_x).astype(jnp.float32)
    is_top = lax.axis_index(LAT) == lax.axis_size(LAT) - 1
    upper_rim = jnp.where(is_top, ghost_row, lat_ext[:, :, :, -1].astype(jnp.float32))
    above = jnp.concatenate(
        [lat_ext[:, :, :, 2:-1].astype(jnp.float32), upper_rim[:, :, :, None]], axis=3
    )
    below = lat_ext[:, :, :, :-2].astype(jnp.float32)
    east_cell = lon_ext[:, :, 2:, :].astype(jnp.float32)
    west_cell = lon_ext[:, :, :-2, :].astype(jnp.float32)
    across = 0.5 * lon_metric * (east_cell - west_cell)
    along = 0.5 * lat_metric * (above - below)
    zeta = across[1] - along[0]
    divergence = across[0] + along[1]
    stacked = (
        jnp.concatenate([zeta, divergence], axis=0).astype(jnp.bfloat16).reshape(columns, cells)
    )
    picked = jnp.take(stacked, wet_index, axis=1)
    live = jnp.arange(cells, dtype=jnp.int32) < wet_count[0]
    snapshot = jnp.where(live[None, :], picked, jnp.zeros_like(picked))
    block_size = min(128, columns)
    block_count = columns // block_size
    gram_one = lax.dot_general(
        snapshot, snapshot, (((1,), (1,)), ((), ())), preferred_element_type=jnp.float32
    )
    first_total = from_blocks(
        sum_by_parts(upper_blocks(gram_one, block_size), (("lat_0", "lat_1"), ("lon_0", "lon_1"))),
        block_count,
    )
    lower_one = jnp.linalg.cholesky(first_total)
    ortho = lax.linalg.triangular_solve(
        lower_one, snapshot.astype(jnp.float32), left_side=True, lower=True
    )
    triangle = lower_one.T
    scale = math.sqrt(cells * lax.axis_size(LAT) * lax.axis_size(LON))
    return ((ortho * scale).astype(jnp.bfloat16), triangle / scale)


def solution(mesh):
    torus = Mesh(mesh.devices.reshape(4, 2, 4, 8), ("lat_0", "lat_1", "lon_0", "lon_1"))
    placed = (P(None, None, LON, LAT), P(LON, LAT), P(LON, LAT), P(LAT_LON), P(LAT_LON))
    return jax.shard_map(
        shards, mesh=torus, in_specs=placed, out_specs=(P(None, LAT_LON), P()), check_vma=False
    )
```

profile of v0, /device:TPU:32, one launch (start us, length us, event | category | flops | bytes accessed | tf_op | source)
XLA Modules:
  0.0 414.7 jit_solution(2099460796664710803)
XLA Ops:
  0.6 11.5 %fusion.60 = (bf16[2,256,48,1]{3,2,1,0:T(8,128)(2,1)}, bf16[2,256,48,1]{3,2,1,0:T(8,128)(2,1)}) fusion(bf16[2,256,48,128]{3,2,1,0:T(8,128)(2,1)} %param.5), kind=kLoop, calls=%fused_computation.135 | loop fusion | bytes 196608 | tf_op jit(solution)/shard_map/slice | solution.py:24
  12.2 7.9 %copy.109 = bf16[2,256,48,1]{1,2,3,0:T(8,128)(2,1)S(1)} copy(bf16[2,256,48,1]{3,2,1,0:T(8,128)(2,1)} %get-tuple-element.39) | data formatting | bytes 98304
  20.1 1.7 collective-permute-start.8
  22.2 1.5 collective-permute-start.2
  23.7 6.1 %copy.110 = bf16[2,256,48,1]{2,1,0,3:T(8,128)(2,1)S(1)} copy(bf16[2,256,48,1]{3,2,1,0:T(8,128)(2,1)} %get-tuple-element.38) | data formatting | bytes 98304
  31.1 2.0 fusion.59
  33.9 1.9 collective-permute-start.1
  35.8 3.6 collective-permute-start.3
  39.4 9.1 %slice_convert_fusion = f32[2,256,48,127]{3,2,1,0:T(8,128)} fusion(bf16[2,256,48,128]{3,2,1,0:T(8,128)(2,1)} %param.5), kind=kLoop, calls=%fused_computation.29 | loop fusion | flops 3121152 | bytes 18726912 | tf_op jit(solution)/shard_map/convert_element_type | solution.py:139
  48.4 5.5 %collective-permute-start.4 = (bf16[24576]{0:T(1024)(128)(2,1)S(1)}, bf16[24576]{0:T(1024)(128)(2,1)S(1)}, u32[]{:S(2)}, u32[]{:S(2)}) collective-permute-start(bf16[24576]{0:T(1024)(128)(2,1)S(1)} %collective-permute-done.3), channel_id=1, source_target_pairs={{0,4},{4,0},{1,5},{5,1},{2,6},{6,2},{3,7},{7,3},{8,12},{12,8},{9,1... | collective-permute-start | bytes 147464 | tf_op jit(solution)/shard_map/ppermute | solution.py:36
  53.9 3.2 collective-permute-done.4
  57.1 1.6 collective-permute-start.5
  59.3 1.8 collective-permute-done.5
  61.2 4.0 collective-permute-start.6
  65.1 6.7 %copy.89 = bf16[2,256,48,1]{3,2,1,0:T(8,128)(2,1)} copy(bf16[2,256,48,1]{1,2,3,0:T(8,128)(2,1)S(1)} %collective-permute-done.8) | data formatting | bytes 98304 | tf_op jit(solution)/shard_map/ppermute | solution.py:21
  72.5 7.1 %copy.88 = f32[2,256,48,1]{3,2,1,0:T(8,128)} copy(f32[2,256,48,1]{2,1,0,3:T(8,128)S(1)} %convert_select_fusion) | data formatting | bytes 196608 | tf_op jit(solution)/shard_map/jit(_where)/select_n | solution.py:137
  79.6 26.5 %subtract_multiply_fusion = (f32[2,256,48,128]{3,2,1,0:T(8,128)S(1)}, f32[2,256,48,128]{3,2,1,0:T(8,128)}) fusion(bf16[2,256,48,128]{3,2,1,0:T(8,128)(2,1)} %param.5, bf16[2,256,1,128]{3,2,1,0:T(2,128)(2,1)S(1)} %copy.84, bf16[2,256,1,128]{3,2,1,0:T(2,128)(2,1)S(1)} %copy.82, f32[48,128]{1,0:T(8,128)S(1)} %get-tuple-element.70, ...), kind=kLoop, calls=%fused_computation.7 | loop fusion | flops 53477376 | bytes 44400640 | tf_op jit(solution)/shard_map/mul | solution.py:144
  106.1 7.1 %fusion.12 = (bf16[1,256,48,128]{3,2,1,0:T(8,128)(2,1)}, bf16[1,256,48,128]{3,2,1,0:T(8,128)(2,1)}) fusion(f32[2,256,48,128]{3,2,1,0:T(8,128)} %get-tuple-element.35, f32[2,256,48,128]{3,2,1,0:T(8,128)S(1)} %get-tuple-element.34), kind=kLoop, calls=%fused_computation.20 | loop fusion | flops 6291456 | bytes 31457280 | tf_op jit(solution)/shard_map/convert.3
  113.3 3.9 copy.90
  117.2 5.0 %copy.91 = bf16[1,256,48,128]{1,3,2,0:T(8,128)(2,1)} copy(bf16[1,256,48,128]{3,2,1,0:T(8,128)(2,1)} %get-tuple-element.33) | data formatting | bytes 6291456 | tf_op jit(solution)/shard_map/convert.2
  122.2 5.0 %pad_maximum_fusion.3 = bf16[512,6144]{0,1:T(8,128)(2,1)} fusion(bf16[256,6144]{0,1:T(8,128)(2,1)} %bitcast.138, bf16[256,6144]{0,1:T(8,128)(2,1)S(1)} %bitcast.137), kind=kLoop, calls=%fused_computation.24 | loop fusion | flops 12582912 | bytes 12582912 | tf_op jit(solution)/shard_map/concatenate | solution.py:149
  127.2 29.3 %gather_fusion = bf16[6144,512]{1,0:T(8,128)(2,1)} fusion(bf16[512,6144]{0,1:T(8,128)(2,1)} %pad_maximum_fusion.3, s32[6144]{0:T(1024)S(1)} %fusion.51), kind=kCustom, calls=%fused_computation | custom fusion | bytes 12607488 | tf_op jit(solution)/shard_map/jit(_take)/gather | solution.py:151
  156.5 8.6 %copy.92 = bf16[6144,512]{0,1:T(8,128)(2,1)} copy(bf16[6144,512]{1,0:T(8,128)(2,1)} %gather_fusion) | data formatting | bytes 12582912 | tf_op jit(solution)/shard_map/jit(_take)/gather | solution.py:151
  165.1 8.5 %fusion.16 = f32[512,512]{1,0:T(8,128)S(1)} fusion(bf16[6144,512]{0,1:T(8,128)(2,1)} %copy.92, pred[6144]{0:T(1024)(128)(4,1)S(1)} %get-tuple-element.71, pred[6144]{0:T(1024)(128)(4,1)S(1)} %get-tuple-element.72), kind=kOutput, calls=%fused_computation.30 | convolution fusion | flops 3227516928 | bytes 7352320 | tf_op jit(solution)/shard_map/dot_general | solution.py:156
  174.3 28.2 %all_to_all.20 = f32[32,8,5,128]{3,1,2,0:T(8,128)S(1)} all-to-all(f32[32,8,5,128]{3,1,2,0:T(8,128)S(1)} %copy.93), channel_id=1, replica_groups=mesh['lat_0'=4,'lat_1'=2,'lon_0'=4,'lon_1'=8] {'lon_0','lon_1'}, dimensions={0} | all-to-all | bytes 1310720 | tf_op jit(solution)/shard_map/all_to_all | solution.py:46
  202.6 8.1 %all_to_all.21 = f32[8,5,128]{2,1,0:T(8,128)S(1)} all-to-all(f32[8,5,128]{2,1,0:T(8,128)S(1)} %copy.94), channel_id=1, replica_groups=mesh['lat_0'=4,'lat_1'=2,'lon_0'=4,'lon_1'=8] {'lat_0','lat_1'}, dimensions={0} | all-to-all | bytes 40960 | tf_op jit(solution)/shard_map/all_to_all | solution.py:54
  211.4 3.3 all-to-all-start.2
  214.8 5.3 %all-to-all-done.2 = f32[8,5,128]{2,1,0:T(8,128)S(1)} async-done(((f32[8,5,128]{2,1,0:T(8,128)}), f32[8,5,128]{2,1,0:T(8,128)S(1)}, u32[]{:S(2)}, u32[]{:S(2)}) %all-to-all-start.2) | async-done | bytes 20512 | tf_op jit(solution)/shard_map/all_to_all | solution.py:67
  221.0 5.0 %all-to-all-start.3 = ((f32[32,8,5,128]{3,1,2,0:T(8,128)}), f32[32,8,5,128]{3,1,2,0:T(8,128)S(1)}, u32[]{:S(2)}, u32[]{:S(2)}) async-start(f32[32,8,5,128]{3,1,2,0:T(8,128)} %broadcast_in_dim.47), calls=%async_computation.3 | async-start | bytes 1310720 | tf_op jit(solution)/shard_map/all_to_all | solution.py:67
  226.0 10.8 %fusion.56 = (f32[512,6144]{1,0:T(8,128)}, bf16[512,6144]{1,0:T(8,128)(2,1)}) fusion(bf16[6144,512]{0,1:T(8,128)(2,1)} %copy.92, pred[6144]{0:T(1024)(128)(4,1)S(1)} %get-tuple-element.72, pred[6144]{0:T(1024)(128)(4,1)S(1)} %get-tuple-element.71), kind=kLoop, calls=%fused_computation.132 | loop fusion | flops 9437184 | bytes 25178112 | tf_op jit(solution)/shard_map/convert_element_type | solution.py:165
  236.8 9.2 %all-to-all-done.3 = f32[32,8,5,128]{3,1,2,0:T(8,128)S(1)} async-done(((f32[32,8,5,128]{3,1,2,0:T(8,128)}), f32[32,8,5,128]{3,1,2,0:T(8,128)S(1)}, u32[]{:S(2)}, u32[]{:S(2)}) %all-to-all-start.3) | async-done | bytes 655392 | tf_op jit(solution)/shard_map/all_to_all | solution.py:67
  247.8 11.7 %cholesky.104 = f32[128,128]{1,0:T(8,128)S(1)} custom-call(f32[128,128]{1,0:T(8,128)S(1)} %cholesky.266), custom_call_target="Cholesky" | custom-call | tf_op jit(solution)/shard_map/jit(cholesky)/cholesky | solution.py:163
  259.7 9.8 %custom-call.30 = f32[1,128,128]{1,2,0:T(8,128)S(1)} custom-call(f32[1,128,128]{2,1,0:T(8,128)S(1)} %get-tuple-element.66), custom_call_target="InvertDiagBlocksLowerTriangular" | custom-call | tf_op jit(solution)/shard_map/jit(cholesky)/cholesky | solution.py:163
  270.2 12.1 %cholesky.217 = f32[128,128]{1,0:T(8,128)S(1)} custom-call(f32[128,128]{1,0:T(8,128)S(1)} %cholesky.270), custom_call_target="Cholesky" | custom-call | tf_op jit(solution)/shard_map/jit(cholesky)/cholesky | solution.py:163
  283.6 9.8 %custom-call.31 = f32[1,128,128]{1,2,0:T(8,128)S(1)} custom-call(f32[1,128,128]{2,1,0:T(8,128)S(1)} %get-tuple-element.63), custom_call_target="InvertDiagBlocksLowerTriangular" | custom-call | tf_op jit(solution)/shard_map/jit(cholesky)/cholesky | solution.py:163
  294.1 11.7 %cholesky.238 = f32[128,128]{1,0:T(8,128)S(1)} custom-call(f32[128,128]{1,0:T(8,128)S(1)} %cholesky.275), custom_call_target="Cholesky" | custom-call | tf_op jit(solution)/shard_map/jit(cholesky)/cholesky | solution.py:163
  306.5 9.8 %custom-call.32 = f32[1,128,128]{1,2,0:T(8,128)S(1)} custom-call(f32[1,128,128]{2,1,0:T(8,128)S(1)} %get-tuple-element.60), custom_call_target="InvertDiagBlocksLowerTriangular" | custom-call | tf_op jit(solution)/shard_map/jit(cholesky)/cholesky | solution.py:163
  317.0 11.9 %cholesky.255 = f32[128,128]{1,0:T(8,128)S(1)} custom-call(f32[128,128]{1,0:T(8,128)S(1)} %convolution_subtract_fusion.4), custom_call_target="Cholesky" | custom-call | tf_op jit(solution)/shard_map/jit(cholesky)/cholesky | solution.py:163
  332.2 8.1 %while.1 = (s32[]{:T(128)}, f32[512,512]{1,0:T(8,128)S(1)}, s32[4,2]{0,1:T(2,128)S(1)}, f32[4,128,128]{2,1,0:T(8,128)S(1)}, s32[]{:T(128)}) while((s32[]{:T(128)}, f32[512,512]{1,0:T(8,128)S(1)}, s32[4,2]{0,1:T(2,128)S(1)}, f32[4,128,128]{2,1,0:T(8,128)S(1)}, s32[]{:T(128)}) %tuple.57), condition=%wide.while_cond, body=%wide.while_body.sunk | while | flops 2 | bytes 131181 | solution.py:164
  340.3 39.3 %custom-call.33 = f32[4,128,128]{1,2,0:T(8,128)S(1)} custom-call(f32[4,128,128]{2,1,0:T(8,128)S(1)} %get-tuple-element.9), custom_call_target="InvertDiagBlocksLowerTriangular" | custom-call | tf_op jit(solution)/shard_map/triangular_solve | solution.py:164
  379.6 2.8 fusion.20
  382.4 4.9 %convolution_subtract_fusion = f32[128,6144]{1,0:T(8,128)S(1)} fusion(f32[128,6144]{1,0:T(8,128)S(1)} %fusion.20, f32[512,6144]{1,0:T(8,128)} %get-tuple-element.28, f32[512,512]{1,0:T(8,128)S(1)} %get-tuple-element.117), kind=kOutput, calls=%fused_computation.14 | convolution fusion | flops 1208745984 | bytes 9502720 | tf_op jit(solution)/shard_map/triangular_solve | solution.py:164
  387.3 2.9 fusion.35
  390.2 5.9 %convolution_subtract_fusion.1 = f32[128,6144]{1,0:T(8,128)S(1)} fusion(f32[128,6144]{1,0:T(8,128)S(1)} %fusion.35, f32[128,6144]{1,0:T(8,128)S(1)} %fusion.20, f32[512,6144]{1,0:T(8,128)} %get-tuple-element.28, f32[512,512]{1,0:T(8,128)S(1)} %get-tuple-element.117), kind=kOutput, calls=%fused_computation.15 | convolution fusion | flops 2418278400 | bytes 12713984 | tf_op jit(solution)/shard_map/triangular_solve | solution.py:164
  396.2 3.1 fusion.33
  399.3 7.3 %fusion.8 = f32[128,6144]{1,0:T(8,128)S(1)} fusion(f32[128,6144]{1,0:T(8,128)S(1)} %fusion.33, f32[128,6144]{1,0:T(8,128)S(1)} %fusion.35, f32[128,6144]{1,0:T(8,128)S(1)} %fusion.20, f32[512,6144]{1,0:T(8,128)} %get-tuple-element.28, f32[512,512]{1,0:T(8,128)S(1)} %get-tuple-element.117), kind=kOutput, calls=%fused_computation.16 | convolution fusion | flops 3629383680 | bytes 15925248 | tf_op jit(solution)/shard_map/triangular_solve | solution.py:164
  406.6 2.8 fusion.32
  409.4 3.7 fusion.1
  (96 shorter events, 21.3 us)
Async XLA Ops:
  20.1 45.1 %collective-permute-start.8 = (bf16[2,256,48,1]{1,2,3,0:T(8,128)(2,1)S(1)}, bf16[2,256,48,1]{1,2,3,0:T(8,128)(2,1)S(1)}, u32[]{:S(2)}, u32[]{:S(2)}) collective-permute-start(bf16[2,256,48,1]{1,2,3,0:T(8,128)(2,1)S(1)} %copy.109), channel_id=1, source_target_pairs={{0,32},{32,64},{64,96},{96,128},{128,160},{160,192},{192,224},{1,3... | collective-permute-start | bytes 147464 | tf_op jit(solution)/shard_map/ppermute | solution.py:21
  22.2 13.5 %collective-permute-start.2 = (bf16[24576]{0:T(1024)(128)(2,1)S(1)}, bf16[24576]{0:T(1024)(128)(2,1)S(1)}, u32[]{:S(2)}, u32[]{:S(2)}) collective-permute-start(bf16[24576]{0:T(1024)(128)(2,1)S(1)} %reshape_squeeze.3), channel_id=1, source_target_pairs={{0,1},{1,0},{2,3},{3,2},{4,5},{5,4},{6,7},{7,6},{8,9},{9,8},{10,11... | collective-permute-start | bytes 147464 | tf_op jit(solution)/shard_map/ppermute | solution.py:36
  29.8 42.7 %collective-permute-start.7 = (bf16[2,256,48,1]{2,1,0,3:T(8,128)(2,1)S(1)}, bf16[2,256,48,1]{2,1,0,3:T(8,128)(2,1)S(1)}, u32[]{:S(2)}, u32[]{:S(2)}) collective-permute-start(bf16[2,256,48,1]{2,1,0,3:T(8,128)(2,1)S(1)} %copy.110), channel_id=1, source_target_pairs={{32,0},{64,32},{96,64},{128,96},{160,128},{192,160},{224,192},{33,... | collective-permute-start | bytes 147464 | tf_op jit(solution)/shard_map/ppermute | solution.py:24
  33.1 38.8 %collective-permute-start = (bf16[2,256,1,128]{3,1,2,0:T(8,128)(2,1)S(1)}, bf16[2,256,1,128]{3,1,2,0:T(8,128)(2,1)S(1)}, u32[]{:S(2)}, u32[]{:S(2)}) collective-permute-start(bf16[2,256,1,128]{3,1,2,0:T(8,128)(2,1)S(1)} %copy.107), channel_id=1, source_target_pairs={{1,0},{2,1},{3,2},{4,3},{5,4},{6,5},{7,6},{8,7},{9,8},{10,9},{11,1... | collective-permute-start | bytes 393224 | tf_op jit(solution)/shard_map/ppermute | solution.py:24
  33.8 20.1 %copy-start.1 = (f32[48,128]{1,0:T(8,128)S(1)}, f32[48,128]{1,0:T(8,128)}, u32[]{:S(2)}) copy-start(f32[48,128]{1,0:T(8,128)} %param.7) | copy-start | bytes 73732
  33.8 20.1 %copy-start.2 = (f32[48,128]{1,0:T(8,128)S(1)}, f32[48,128]{1,0:T(8,128)}, u32[]{:S(2)}) copy-start(f32[48,128]{1,0:T(8,128)} %param.6) | copy-start | bytes 73732
  33.9 24.8 %copy-start = (s32[6144]{0:T(1024)S(1)}, s32[6144]{0:T(1024)}, u32[]{:S(2)}) copy-start(s32[6144]{0:T(1024)} %param.8) | copy-start | bytes 73732
  33.9 38.2 %collective-permute-start.1 = (bf16[2,256,1,128]{3,1,2,0:T(8,128)(2,1)S(1)}, bf16[2,256,1,128]{3,1,2,0:T(8,128)(2,1)S(1)}, u32[]{:S(2)}, u32[]{:S(2)}) collective-permute-start(bf16[2,256,1,128]{3,1,2,0:T(8,128)(2,1)S(1)} %copy.108), channel_id=1, source_target_pairs={{0,1},{1,2},{2,3},{3,4},{4,5},{5,6},{6,7},{7,8},{8,9},{9,10},{10,1... | collective-permute-start | bytes 393224 | tf_op jit(solution)/shard_map/ppermute | solution.py:21
  35.8 12.6 %collective-permute-start.3 = (bf16[24576]{0:T(1024)(128)(2,1)S(1)}, bf16[24576]{0:T(1024)(128)(2,1)S(1)}, u32[]{:S(2)}, u32[]{:S(2)}) collective-permute-start(bf16[24576]{0:T(1024)(128)(2,1)S(1)} %collective-permute-done.2), channel_id=1, source_target_pairs={{0,2},{2,0},{1,3},{3,1},{4,6},{6,4},{5,7},{7,5},{8,10},{10,8},{9,1... | collective-permute-start | bytes 147464 | tf_op jit(solution)/shard_map/ppermute | solution.py:36
  48.4 8.6 %collective-permute-start.4 = (bf16[24576]{0:T(1024)(128)(2,1)S(1)}, bf16[24576]{0:T(1024)(128)(2,1)S(1)}, u32[]{:S(2)}, u32[]{:S(2)}) collective-permute-start(bf16[24576]{0:T(1024)(128)(2,1)S(1)} %collective-permute-done.3), channel_id=1, source_target_pairs={{0,4},{4,0},{1,5},{5,1},{2,6},{6,2},{3,7},{7,3},{8,12},{12,8},{9,1... | collective-permute-start | bytes 147464 | tf_op jit(solution)/shard_map/ppermute | solution.py:36
  57.1 4.1 collective-permute-start.5
  61.2 11.1 %collective-permute-start.6 = (bf16[24576]{0:T(1024)(128)(2,1)S(1)}, bf16[24576]{0:T(1024)(128)(2,1)S(1)}, u32[]{:S(2)}, u32[]{:S(2)}) collective-permute-start(bf16[24576]{0:T(1024)(128)(2,1)S(1)} %collective-permute-done.5), channel_id=1, source_target_pairs={{0,16},{16,0},{1,17},{17,1},{2,18},{18,2},{3,19},{19,3},{4,20},{20... | collective-permute-start | bytes 147464 | tf_op jit(solution)/shard_map/ppermute | solution.py:36
  211.4 8.7 %all-to-all-start.2 = ((f32[8,5,128]{2,1,0:T(8,128)}), f32[8,5,128]{2,1,0:T(8,128)S(1)}, u32[]{:S(2)}, u32[]{:S(2)}) async-start(f32[8,5,128]{2,1,0:T(8,128)} %broadcast_in_dim.46), calls=%async_computation.2 | async-start | bytes 65536 | tf_op jit(solution)/shard_map/all_to_all | solution.py:67
  221.0 25.0 %all-to-all-start.3 = ((f32[32,8,5,128]{3,1,2,0:T(8,128)}), f32[32,8,5,128]{3,1,2,0:T(8,128)S(1)}, u32[]{:S(2)}, u32[]{:S(2)}) async-start(f32[32,8,5,128]{3,1,2,0:T(8,128)} %broadcast_in_dim.47), calls=%async_computation.3 | async-start | bytes 1310720 | tf_op jit(solution)/shard_map/all_to_all | solution.py:67
where the time goes:
time: 423 us; the launch traced here: 415 us
  other arithmetic  182 us (43%)
  local copies, waits for them, and re-layouts  102 us (24%)
  matrix products  40.1 us (9%)
  blocking collectives  36.4 us (9%)
  starting transfers between devices  30 us (7%)
  waiting for transfers between devices  19.6 us (5%)
  between operations  4.58 us (1%)
    another operation x15, other arithmetic, shards(): lower_one = jnp.linalg.cholesky(first_total)  79.5 us
    another operation x2, other arithmetic, shards(): lax.linalg.triangular_solve(lower_one, snapshot.astype(jnp.float32), left...  39.3 us
    gather x2, local copies, waits for them, and re-layouts, shards(): picked = jnp.take(stacked, wet_index, axis=1)  37.9 us
    another operation x7, matrix products, shards(): lax.linalg.triangular_solve(lower_one, snapshot.astype(jnp.float32), left...  29.8 us
    all_to_all x1, blocking collectives, sent_and_summed(): lax.all_to_all(parts, axis, split_axis=0, concat_axis=0, tiled=True)  28.2 us
    mul x1, other arithmetic, shards(): across = 0.5 * lon_metric * (east_cell - west_cell)  26.5 us
    another operation x14, local copies, waits for them, and re-layouts  16.9 us
    ppermute x5, starting transfers between devices, partner(): return lax.ppermute(block, axis, route)  16 us
  transfers between devices with their start and end apart: 11, of which 4 were waited for; matrix products, arithmetic and copies ran while one was open for 9% of the time, Pallas kernels for 0%

commit v1 on v0

v1 whole, which is shorter than its diff:
```python
import functools
import math

import jax
import jax.numpy as jnp
from jax import lax
from jax.experimental import pallas as pl
from jax.experimental.pallas import tpu as pltpu
from jax.sharding import PartitionSpec as P

MESH = pl.DeviceIdType.MESH
VMEM = pl.BlockSpec(memory_space=pltpu.VMEM)
SMEM = pl.BlockSpec(memory_space=pltpu.SMEM)
ANY = pl.BlockSpec(memory_space=pl.ANY)
BIG = 60 << 20
NT = (((1,), (1,)), ((), ()))
TN = (((0,), (0,)), ((), ()))
NN = (((1,), (0,)), ((), ()))


def metric_kernel(idx_ref, count_ref, lon_ref, lat_ref, lon_out, lat_out):
    count = count_ref[0]
    pieces, width = idx_ref.shape
    nx, ny = lon_ref.shape
    total = jnp.zeros((nx, ny), jnp.float32)
    for at in range(pieces):
        cell = idx_ref[at : at + 1, :]
        place = lax.broadcasted_iota(jnp.int32, (1, width), 1) + at * width
        column = jnp.where(place < count, cell // ny, -1)
        row = cell % ny
        hot_x = (lax.broadcasted_iota(jnp.int32, (nx, width), 0) == column).astype(jnp.float32)
        hot_y = (lax.broadcasted_iota(jnp.int32, (ny, width), 0) == row).astype(jnp.float32)
        total += lax.dot_general(
            hot_x.astype(jnp.bfloat16),
            hot_y.astype(jnp.bfloat16),
            NT,
            preferred_element_type=jnp.float32,
        )
    lon_out[...] = 0.5 * lon_ref[...] * total
    lat_out[...] = 0.5 * lat_ref[...] * total


def turn_kernel(v_ref, o_ref, north_ref, south_ref, scr):
    scr[...] = v_ref[...].astype(jnp.float32)
    for x in range(v_ref.shape[1]):
        turned = scr[:, x, :].T
        o_ref[x] = turned.astype(jnp.bfloat16)
        north_ref[x : x + 1, :] = turned[-1:, :]
        south_ref[x : x + 1, :] = turned[:1, :]


def halo_kernel(n_lat, n_lon, vt, north_edge, south_edge, west, east, south, north, send, recv):
    lat, lon = lax.axis_index("lat"), lax.axis_index("lon")
    last = vt.shape[0] - 1
    right = (lat, lax.rem(lon + 1, n_lon))
    left = (lat, lax.rem(lon + n_lon - 1, n_lon))
    is_top = lat == n_lat - 1
    up = (jnp.where(is_top, lat, lat + 1), jnp.where(is_top, n_lon - 1 - lon, lon))
    down = (jnp.where(lat == 0, lat, lat - 1), lon)
    barrier = pltpu.get_barrier_semaphore()
    for other in (right, left, up):
        pl.semaphore_signal(barrier, inc=1, device_id=other, device_id_type=MESH)

    @pl.when(lat > 0)
    def _():
        pl.semaphore_signal(barrier, inc=1, device_id=down, device_id_type=MESH)

    pl.semaphore_wait(barrier, jnp.where(lat > 0, 4, 3))

    def copy(src, dst, slot, to):
        return pltpu.make_async_remote_copy(
            src_ref=src,
            dst_ref=dst,
            send_sem=send.at[slot],
            recv_sem=recv.at[slot],
            device_id=to,
            device_id_type=MESH,
        )

    to_right = copy(vt.at[last], west, 0, right)
    to_left = copy(vt.at[0], east, 1, left)
    to_up = copy(north_edge, south, 2, up)
    to_fold = copy(north_edge, north, 3, up)

    @pl.when(is_top)
    def _():
        to_fold.start()

    @pl.when(jnp.logical_not(is_top))
    def _():
        to_up.start()

    @pl.when(lat > 0)
    def _():
        to_down_other = pltpu.make_async_remote_copy(
            src_ref=south_edge,
            dst_ref=north,
            send_sem=send.at[4],
            recv_sem=recv.at[3],
            device_id=down,
            device_id_type=MESH,
        )
        to_down_other.start()

    to_right.start()
    to_left.start()

    @pl.when(lat == 0)
    def _():
        south[...] = jnp.zeros_like(south)

    @pl.when(lat > 0)
    def _():
        to_up.wait_recv()

    to_fold.wait_recv()
    to_right.wait_recv()
    to_left.wait_recv()
    to_right.wait_send()
    to_left.wait_send()

    @pl.when(is_top)
    def _():
        to_fold.wait_send()

    @pl.when(jnp.logical_not(is_top))
    def _():
        to_up.wait_send()

    @pl.when(lat > 0)
    def _():
        pltpu.make_async_remote_copy(
            src_ref=south_edge,
            dst_ref=north,
            send_sem=send.at[4],
            recv_sem=recv.at[3],
            device_id=down,
            device_id_type=MESH,
        ).wait_send()


def field_kernel(
    top_ref, vt, before, after, west, east, south, north, lon_m, lat_m, f_ref, gram_ref, scr
):
    step = pl.program_id(0)
    steps = pl.num_programs(0)
    width, ny, columns = vt.shape
    half = columns // 2
    is_top = top_ref[0] == 1
    lon_t = lon_m[...].T
    lat_t = lat_m[...].T
    row = lax.broadcasted_iota(jnp.int32, (ny, 1), 0)
    iy = lax.broadcasted_iota(jnp.int32, (ny, ny), 0)
    ix = lax.broadcasted_iota(jnp.int32, (ny, ny), 1)
    band = (ix == iy + 1).astype(jnp.float32) - (ix == iy - 1).astype(jnp.float32)
    band = band.astype(jnp.bfloat16)
    nx = width * 3
    for at in range(width):
        x = step * width + at
        if at == 0:
            lower = jnp.where(step == 0, west[...], before[0])
        else:
            lower = vt[at - 1]
        if at == width - 1:
            upper = jnp.where(step == steps - 1, east[...], after[0])
        else:
            upper = vt[at + 1]
        over_x = upper.astype(jnp.float32) - lower.astype(jnp.float32)
        x_top = jnp.where(is_top, nx - 1 - x, x)
        above = north[pl.ds(x_top, 1), :]
        above = jnp.where(is_top, -above, above)
        below = south[pl.ds(x, 1), :]
        over_y = lax.dot_general(band, vt[at], NN, preferred_element_type=jnp.float32)
        over_y = over_y + jnp.where(row == ny - 1, above, 0.0) - jnp.where(row == 0, below, 0.0)
        m_lon = lon_t[:, at : at + 1]
        m_lat = lat_t[:, at : at + 1]
        zeta = m_lon * over_x[:, half:] - m_lat * over_y[:, :half]
        divergence = m_lon * over_x[:, :half] + m_lat * over_y[:, half:]
        f_ref[at * ny : (at + 1) * ny, :half] = zeta.astype(jnp.bfloat16)
        f_ref[at * ny : (at + 1) * ny, half:] = divergence.astype(jnp.bfloat16)
    part = lax.dot_general(f_ref[...], f_ref[...], TN, preferred_element_type=jnp.float32)

    @pl.when(step == 0)
    def _():
        scr[...] = part

    @pl.when(step > 0)
    def _():
        scr[...] += part

    @pl.when(step == steps - 1)
    def _():
        at = 0
        for i in range(4):
            for j in range(i, 4):
                gram_ref[at] = scr[i * 128 : (i + 1) * 128, j * 128 : (j + 1) * 128]
                at += 1


def sum_kernel(g, out, r0, s0, r1, r2, s1, r3, send0, recv0, send1, recv1, send2, recv2, send3, recv3, send4, recv4):
    lat, lon = lax.axis_index("lat"), lax.axis_index("lon")
    core, cx = lax.rem(lat, 2), lat // 2
    cy, cz = lon // 8, lax.rem(lon, 8)
    mine = cx * 4 + cy
    mate = (lat + 1 - 2 * core, lon)

    def plane(off):
        spot = lax.rem(mine + off, 16)
        return spot, (2 * (spot // 4) + core, 8 * lax.rem(spot, 4) + cz)

    def column(off):
        return (lat, 8 * cy + lax.rem(cz + off, 8))

    barrier = pltpu.get_barrier_semaphore()
    pl.semaphore_signal(barrier, inc=1, device_id=mate, device_id_type=MESH)
    for off in range(1, 16):
        pl.semaphore_signal(barrier, inc=1, device_id=plane(off)[1], device_id_type=MESH)
    for off in range(1, 8):
        pl.semaphore_signal(barrier, inc=1, device_id=column(off), device_id_type=MESH)
    pl.semaphore_wait(barrier, 23)

    def copy(src, dst, send, recv, to):
        return pltpu.make_async_remote_copy(
            src_ref=src, dst_ref=dst, send_sem=send, recv_sem=recv, device_id=to, device_id_type=MESH
        )

    first = copy(g.at[1 - core], r0, send0.at[0], recv0.at[0], mate)
    first.start()
    first.wait_recv()
    s0[...] = g[core] + r0[...]
    second = []
    for off in range(1, 16):
        spot, to = plane(off)
        second.append(copy(s0.at[spot], r1.at[mine], send1.at[off - 1], recv1.at[off - 1], to))
        second[-1].start()
    r1[mine] = s0[mine]
    for item in second:
        item.wait_recv()
    total = r1[0]
    for at in range(1, 16):
        total = total + r1[at]
    s1[0] = total
    r2[cz] = total
    third = []
    for off in range(1, 8):
        third.append(copy(s1.at[0], r2.at[cz], send2.at[off - 1], recv2.at[off - 1], column(off)))
        third[-1].start()
    for item in third:
        item.wait_recv()
    total = r2[0]
    for at in range(1, 8):
        total = total + r2[at]
    s1[1] = total
    r3[mine] = total
    fourth = []
    for off in range(1, 16):
        fourth.append(
            copy(s1.at[1], r3.at[mine], send3.at[off - 1], recv3.at[off - 1], plane(off)[1])
        )
        fourth[-1].start()
    for item in fourth:
        item.wait_recv()
    last = copy(r3, out.at[core], send4.at[0], recv4.at[0], mate)
    last.start()
    out[core] = r3[...]
    last.wait_recv()
    for item in [first, *second, *third, *fourth, last]:
        item.wait_send()


def pick_kernel(idx_ref, f_ref, o_ref, spread, picked):
    rows = f_ref.shape[0]
    lanes = f_ref.shape[1] // 4

    def widen(at, _):
        base = pl.multiple_of(at * 128, 128)
        for k in range(4):
            spread[pl.ds(base, 128), k, :] = f_ref[
                pl.ds(base, 128), k * lanes : (k + 1) * lanes
            ].astype(jnp.float32)
        return 0

    lax.fori_loop(0, rows // 128, widen, 0)

    def pick(at, _):
        base = at * 32
        for u in range(32):
            picked[base + u] = spread[idx_ref[base + u]]
        return 0

    lax.fori_loop(0, rows // 32, pick, 0)

    def narrow(at, _):
        base = pl.multiple_of(at * 128, 128)
        for k in range(4):
            o_ref[pl.ds(base, 128), k * lanes : (k + 1) * lanes] = picked[
                pl.ds(base, 128), k, :
            ].astype(jnp.bfloat16)
        return 0

    lax.fori_loop(0, rows // 128, narrow, 0)


def exact(a, b, dims):
    return lax.dot_general(
        a, b, dims, precision=lax.Precision.HIGHEST, preferred_element_type=jnp.float32
    )


def eliminate(a):
    n = a.shape[0]
    ri = lax.broadcasted_iota(jnp.int32, (n, n), 0)
    ci = lax.broadcasted_iota(jnp.int32, (n, n), 1)
    for k in range(n):
        row = a[k : k + 1, :]
        m = jnp.where(ri[:, :1] > k, a[:, k : k + 1] * (1.0 / a[k : k + 1, k : k + 1]), 0.0)
        rowz = jnp.where(ci[:1] == k, 1.0, row)
        a = jnp.where((ci == k) & (ri > k), 0.0, a) - m * rowz
    diagonal = jnp.sum(jnp.where(ri == ci, a, 0.0), axis=1, keepdims=True)
    root = lax.rsqrt(diagonal)
    upper = jnp.where(ri <= ci, a, 0.0) * root
    inverse = (jnp.where(ri > ci, a, 0.0) + jnp.where(ri == ci, 1.0, 0.0)) * root
    return upper, inverse


def factor_kernel(scale, g_ref, t_hbm, o_hbm, r_ref, rows, w_ref, stage, in_sem, out_sem):
    load = pltpu.make_async_copy(t_hbm, rows, in_sem)
    load.start()
    b = 128
    n = 4
    g = {}
    at = 0
    for i in range(n):
        for j in range(i, n):
            g[i, j] = g_ref[at]
            at += 1
    r, w = {}, {}
    for p in range(n):
        r[p, p], w[p, p] = eliminate(g[p, p])
        for j in range(p + 1, n):
            r[p, j] = exact(w[p, p], g[p, j], NN)
        for i in range(p + 1, n):
            for j in range(i, n):
                g[i, j] = g[i, j] - exact(r[p, i], r[p, j], TN)
    for i in range(n):
        for j in range(i):
            total = exact(r[j, i], w[j, j], TN)
            for k in range(j + 1, i):
                total = total + exact(r[k, i], w[k, j], TN)
            w[i, j] = -exact(w[i, i], total, NN)
    for i in range(n):
        for j in range(n):
            spot = (slice(i * b, (i + 1) * b), slice(j * b, (j + 1) * b))
            r_ref[spot] = r[i, j] * (1.0 / scale) if i <= j else jnp.zeros((b, b), jnp.float32)
            value = w[i, j] * scale if i >= j else jnp.zeros((b, b), jnp.float32)
            high = value.astype(jnp.bfloat16)
            w_ref[(0, *spot)] = high
            w_ref[(1, *spot)] = (value - high.astype(jnp.float32)).astype(jnp.bfloat16)
    load.wait()
    chunk = stage.shape[2]
    pieces = rows.shape[0] // chunk
    outs = []
    for at in range(pieces):
        slot = at % 2
        if at >= 2:
            outs[at - 2].wait()
        part = rows[at * chunk : (at + 1) * chunk, :]
        value = lax.dot_general(w_ref[0], part, NT, preferred_element_type=jnp.float32)
        value += lax.dot_general(w_ref[1], part, NT, preferred_element_type=jnp.float32)
        stage[slot] = value.astype(jnp.bfloat16)
        outs.append(
            pltpu.make_async_copy(
                stage.at[slot], o_hbm.at[:, pl.ds(at * chunk, chunk)], out_sem.at[slot]
            )
        )
        outs[-1].start()
    for item in outs[-2:]:
        item.wait()


def shards(n_lat, n_lon, velocity, lon_metric, lat_metric, wet_index, wet_count):
    days, nx, ny = velocity.shape[1:]
    cols = 2 * days
    cells = nx * ny
    f32, bf16 = jnp.float32, jnp.bfloat16
    shape = jax.ShapeDtypeStruct
    params = pltpu.CompilerParams(vmem_limit_bytes=BIG)

    lon_m, lat_m = pl.pallas_call(
        metric_kernel,
        in_specs=[VMEM, SMEM, VMEM, VMEM],
        out_specs=[VMEM, VMEM],
        out_shape=[shape((nx, ny), f32)] * 2,
        compiler_params=params,
    )(wet_index.reshape(6, -1), wet_count, lon_metric, lat_metric)

    lane = 128
    vt, north_edge, south_edge = pl.pallas_call(
        turn_kernel,
        grid=(cols // lane,),
        in_specs=[pl.BlockSpec((lane, nx, ny), lambda i: (i, 0, 0))],
        out_specs=[
            pl.BlockSpec((nx, ny, lane), lambda i: (0, 0, i)),
            pl.BlockSpec((nx, lane), lambda i: (0, i)),
            pl.BlockSpec((nx, lane), lambda i: (0, i)),
        ],
        out_shape=[shape((nx, ny, cols), bf16), shape((nx, cols), f32), shape((nx, cols), f32)],
        scratch_shapes=[pltpu.VMEM((lane, nx, ny), f32)],
        compiler_params=params,
    )(velocity.reshape(cols, nx, ny))

    west, east, south, north = pl.pallas_call(
        functools.partial(halo_kernel, n_lat, n_lon),
        in_specs=[ANY, ANY, ANY],
        out_specs=[VMEM] * 4,
        out_shape=[shape((ny, cols), bf16)] * 2 + [shape((nx, cols), f32)] * 2,
        scratch_shapes=[pltpu.SemaphoreType.DMA((5,)), pltpu.SemaphoreType.DMA((4,))],
        compiler_params=pltpu.CompilerParams(collective_id=0, has_side_effects=True),
    )(vt, north_edge, south_edge)

    is_top = (lax.axis_index("lat") == n_lat - 1).astype(jnp.int32).reshape(1)
    width = 16
    last = nx - 1
    whole = lambda a: pl.BlockSpec(a.shape, lambda i: (0,) * a.ndim)
    f, gram = pl.pallas_call(
        field_kernel,
        grid=(nx // width,),
        in_specs=[
            SMEM,
            pl.BlockSpec((width, ny, cols), lambda i: (i, 0, 0)),
            pl.BlockSpec((1, ny, cols), lambda i: (jnp.maximum(width * i - 1, 0), 0, 0)),
            pl.BlockSpec((1, ny, cols), lambda i: (jnp.minimum(width * i + width, last), 0, 0)),
            whole(west),
            whole(east),
            whole(south),
            whole(north),
            pl.BlockSpec((width, ny), lambda i: (i, 0)),
            pl.BlockSpec((width, ny), lambda i: (i, 0)),
        ],
        out_specs=[
            pl.BlockSpec((width * ny, cols), lambda i: (i, 0)),
            pl.BlockSpec((10, 128, 128), lambda i: (0, 0, 0)),
        ],
        out_shape=[shape((cells, cols), bf16), shape((10, 128, 128), f32)],
        scratch_shapes=[pltpu.VMEM((cols, cols), f32)],
        compiler_params=params,
    )(is_top, vt, vt, vt, west, east, south, north, lon_m, lat_m)

    dma = pltpu.SemaphoreType.DMA
    total = pl.pallas_call(
        sum_kernel,
        in_specs=[VMEM],
        out_specs=VMEM,
        out_shape=shape((2, 16, 40, 128), f32),
        scratch_shapes=[
            pltpu.VMEM((16, 40, 128), f32),
            pltpu.VMEM((16, 40, 128), f32),
            pltpu.VMEM((16, 40, 128), f32),
            pltpu.VMEM((8, 40, 128), f32),
            pltpu.VMEM((2, 40, 128), f32),
            pltpu.VMEM((16, 40, 128), f32),
            dma((1,)),
            dma((1,)),
            dma((15,)),
            dma((15,)),
            dma((7,)),
            dma((7,)),
            dma((15,)),
            dma((15,)),
            dma((1,)),
            dma((1,)),
        ],
        compiler_params=pltpu.CompilerParams(collective_id=1, has_side_effects=True),
    )(gram.reshape(2, 16, 40, 128))

    picked = pl.pallas_call(
        pick_kernel,
        in_specs=[SMEM, VMEM],
        out_specs=VMEM,
        out_shape=shape((cells, cols), bf16),
        scratch_shapes=[pltpu.VMEM((cells, 4, 128), f32), pltpu.VMEM((cells, 4, 128), f32)],
        compiler_params=params,
    )(wet_index, f)

    scale = math.sqrt(cells * n_lat * n_lon)
    basis, r_factor = pl.pallas_call(
        functools.partial(factor_kernel, scale),
        in_specs=[VMEM, ANY],
        out_specs=[ANY, VMEM],
        out_shape=[shape((cols, cells), bf16), shape((cols, cols), f32)],
        scratch_shapes=[
            pltpu.VMEM((cells, cols), bf16),
            pltpu.VMEM((2, cols, cols), bf16),
            pltpu.VMEM((2, cols, 768), bf16),
            dma(()),
            dma((2,)),
        ],
        compiler_params=params,
    )(total.reshape(10, 128, 128), picked)
    return basis, r_factor


def solution(mesh):
    n_lat, n_lon = mesh.shape["lat"], mesh.shape["lon"]
    placed = (
        P(None, None, "lon", "lat"),
        P("lon", "lat"),
        P("lon", "lat"),
        P(("lat", "lon")),
        P(("lat", "lon")),
    )
    return jax.shard_map(
        functools.partial(shards, n_lat, n_lon),
        mesh=mesh,
        in_specs=placed,
        out_specs=(P(None, ("lat", "lon")), P()),
        check_vma=False,
    )
```

time: 423 us -> 164 us (0.39)
  the two profiles are of different devices: /device:TPU:32 before, /device:TPU:1 now
where the time goes in v1:
time: 164 us
  Pallas kernels  161 us (98%)
    pallas_call x1, Pallas kernels, shards(): pl.pallas_call(functools.partial(factor_kernel, scale), in_specs=[VMEM, A...  58.8 us
    pallas_call x1, Pallas kernels, shards(): pl.pallas_call(pick_kernel, in_specs=[SMEM, VMEM], out_specs=VMEM, out_sh...  33.1 us
    pallas_call x1, Pallas kernels, shards(): pl.pallas_call(sum_kernel, in_specs=[VMEM], out_specs=VMEM, out_shape=sha...  30.4 us
    pallas_call x1, Pallas kernels, shards(): pl.pallas_call(functools.partial(halo_kernel, n_lat, n_lon), in_specs=[AN...  15.7 us
    pallas_call x1, Pallas kernels, shards(): pl.pallas_call(field_kernel, grid=(nx // width,), in_specs=[SMEM, pl.Bloc...  10.4 us
    pallas_call x1, Pallas kernels, shards(): pl.pallas_call(turn_kernel, grid=(cols // lane,), in_specs=[pl.BlockSpec(...  10.2 us

profile of v1, /device:TPU:1, one launch (start us, length us, event | category | flops | bytes accessed | tf_op | source)
XLA Modules:
  0.0 163.6 jit_solution(14282701844645344309)
XLA Ops:
  1.3 1.4 reshape.24.idx_ref
  2.6 2.1 %shard_map.70 = (f32[48,128]{1,0:T(8,128)}, f32[48,128]{1,0:T(8,128)}) custom-call(s32[6,1024]{1,0:T(8,128)} %reshape.24.idx_ref, s32[1]{0:T(128)S(6)} %copy.7.count_ref, f32[48,128]{1,0:T(8,128)} %lon_ref.1, f32[48,128]{1,0:T(8,128)} %lat_ref.1), custom_call_target="tpu_custom_call" | custom-call | tf_op jit(solution)/shard_map/pallas_call | solution.py:389
  4.7 10.2 %shard_map.68 = (bf16[48,128,512]{2,1,0:T(8,128)(2,1)}, f32[48,512]{1,0:T(8,128)}, f32[48,512]{1,0:T(8,128)}) custom-call(bf16[512,48,128]{2,1,0:T(8,128)(2,1)} %bitcast.4), custom_call_target="tpu_custom_call" | custom-call | tf_op jit(solution)/shard_map/pallas_call | solution.py:398
  15.0 15.7 %shard_map.69 = (bf16[128,512]{1,0:T(8,128)(2,1)}, bf16[128,512]{1,0:T(8,128)(2,1)}, f32[48,512]{1,0:T(8,128)}, f32[48,512]{1,0:T(8,128)}) custom-call(bf16[48,128,512]{2,1,0:T(8,128)(2,1)} %get-tuple-element.13.vt.before.after, f32[48,512]{1,0:T(8,128)} %get-tuple-element.14.north_edge, f32[48,512]{1,0:T(8,128)} %get-tuple-element.15.south_edge), custom_call_target="tpu_custom_call" | custom-call | tf_op jit(solution)/shard_map/pallas_call | solution.py:412
  30.6 10.4 %shard_map.71 = (bf16[6144,512]{1,0:T(8,128)(2,1)}, f32[10,128,128]{2,1,0:T(8,128)}) custom-call(s32[1]{0:T(128)} %bitcast.top_ref, bf16[48,128,512]{2,1,0:T(8,128)(2,1)} %get-tuple-element.13.vt.before.after, bf16[48,128,512]{2,1,0:T(8,128)(2,1)} %get-tuple-element.13.vt.before.after, bf16[48,128,512]{2,1,0:T(8,128)(2,1)} %get-tuple-element.13.vt.before.after, ...), custom_call_target="tpu_custom_call" | custom-call | tf_op jit(solution)/shard_map/pallas_call | solution.py:425
  41.0 30.4 %shard_map.72 = f32[2,16,40,128]{3,2,1,0:T(8,128)} custom-call(f32[2,16,40,128]{3,2,1,0:T(8,128)} %bitcast.6), custom_call_target="tpu_custom_call" | custom-call | tf_op jit(solution)/shard_map/pallas_call | solution.py:450
  71.4 33.1 %shard_map.73.t_hbm = bf16[6144,512]{1,0:T(8,128)(2,1)} custom-call(s32[6144]{0:T(1024)} %idx_ref.1, bf16[6144,512]{1,0:T(8,128)(2,1)} %get-tuple-element.23.f_ref), custom_call_target="tpu_custom_call" | custom-call | tf_op jit(solution)/shard_map/pallas_call | solution.py:476
  104.5 58.8 %shard_map.74 = (bf16[512,6144]{1,0:T(8,128)(2,1)}, f32[512,512]{1,0:T(8,128)}) custom-call(f32[10,128,128]{2,1,0:T(8,128)} %bitcast.5, bf16[6144,512]{1,0:T(8,128)(2,1)} %shard_map.73.t_hbm), custom_call_target="tpu_custom_call" | custom-call | tf_op jit(solution)/shard_map/pallas_call | solution.py:486

commit v2 on v1

--- a/solution.py
+++ b/solution.py
@@ -197,12 +197,17 @@
                 at += 1
 
 
-def sum_kernel(g, out, r0, s0, r1, r2, s1, r3, send0, recv0, send1, recv1, send2, recv2, send3, recv3, send4, recv4):
+def sum_kernel(
+    idx, g, f_hbm, out, t_hbm, rows, spread, picked, r0, s0, r1, r2, s1, r3,
+    send0, recv0, send1, recv1, send2, recv2, send3, recv3, send4, recv4, load_sem, store_sem,
+):
     lat, lon = lax.axis_index("lat"), lax.axis_index("lon")
     core, cx = lax.rem(lat, 2), lat // 2
     cy, cz = lon // 8, lax.rem(lon, 8)
     mine = cx * 4 + cy
     mate = (lat + 1 - 2 * core, lon)
+    cells, cols = rows.shape
+    piece = cells // 4
 
     def plane(off):
         spot = lax.rem(mine + off, 16)
@@ -211,6 +216,35 @@
     def column(off):
         return (lat, 8 * cy + lax.rem(cz + off, 8))
 
+    def widen(at, _):
+        here = pl.ds(pl.multiple_of(at * 128, 128), 128)
+        spread[here] = rows[here, :].astype(jnp.float32).reshape(128, 4, cols // 4)
+        return 0
+
+    def pick(at, _):
+        base = at * 64
+        taken = [spread[idx[base + u]] for u in range(64)]
+        for u in range(64):
+            picked[base + u] = taken[u]
+        return 0
+
+    def narrow(at, _):
+        here = pl.ds(pl.multiple_of(at * 128, 128), 128)
+        rows[here, :] = picked[here].reshape(128, cols).astype(jnp.bfloat16)
+        return 0
+
+    def pick_piece(at):
+        lax.fori_loop(at * piece // 64, (at + 1) * piece // 64, pick, 0)
+
+    def store_piece(at):
+        lax.fori_loop(at * piece // 128, (at + 1) * piece // 128, narrow, 0)
+        here = pl.ds(at * piece, piece)
+        item = pltpu.make_async_copy(rows.at[here], t_hbm.at[here], store_sem.at[at])
+        item.start()
+        return item
+
+    load = pltpu.make_async_copy(f_hbm, rows, load_sem)
+    load.start()
     barrier = pltpu.get_barrier_semaphore()
     pl.semaphore_signal(barrier, inc=1, device_id=mate, device_id_type=MESH)
     for off in range(1, 16):
@@ -234,6 +268,9 @@
         second.append(copy(s0.at[spot], r1.at[mine], send1.at[off - 1], recv1.at[off - 1], to))
         second[-1].start()
     r1[mine] = s0[mine]
+    load.wait()
+    lax.fori_loop(0, cells // 128, widen, 0)
+    pick_piece(0)
     for item in second:
         item.wait_recv()
     total = r1[0]
@@ -245,6 +282,8 @@
     for off in range(1, 8):
         third.append(copy(s1.at[0], r2.at[cz], send2.at[off - 1], recv2.at[off - 1], column(off)))
         third[-1].start()
+    pick_piece(1)
+    pick_piece(2)
     for item in third:
         item.wait_recv()
     total = r2[0]
@@ -258,47 +297,18 @@
             copy(s1.at[1], r3.at[mine], send3.at[off - 1], recv3.at[off - 1], plane(off)[1])
         )
         fourth[-1].start()
+    pick_piece(3)
+    stores = [store_piece(at) for at in range(4)]
     for item in fourth:
         item.wait_recv()
     last = copy(r3, out.at[core], send4.at[0], recv4.at[0], mate)
     last.start()
     out[core] = r3[...]
     last.wait_recv()
+    for item in stores:
+        item.wait()
     for item in [first, *second, *third, *fourth, last]:
         item.wait_send()
-
-
-def pick_kernel(idx_ref, f_ref, o_ref, spread, picked):
-    rows = f_ref.shape[0]
-    lanes = f_ref.shape[1] // 4
-
-    def widen(at, _):
-        base = pl.multiple_of(at * 128, 128)
-        for k in range(4):
-            spread[pl.ds(base, 128), k, :] = f_ref[
-                pl.ds(base, 128), k * lanes : (k + 1) * lanes
-            ].astype(jnp.float32)
-        return 0
-
-    lax.fori_loop(0, rows // 128, widen, 0)
-
-    def pick(at, _):
-        base = at * 32
-        for u in range(32):
-            picked[base + u] = spread[idx_ref[base + u]]
-        return 0
-
-    lax.fori_loop(0, rows // 32, pick, 0)
-
-    def narrow(at, _):
-        base = pl.multiple_of(at * 128, 128)
-        for k in range(4):
-            o_ref[pl.ds(base, 128), k * lanes : (k + 1) * lanes] = picked[
-                pl.ds(base, 128), k, :
-            ].astype(jnp.bfloat16)
-        return 0
-
-    lax.fori_loop(0, rows // 128, narrow, 0)
 
 
 def exact(a, b, dims):
@@ -307,20 +317,79 @@
     )
 
 
+def tree(terms):
+    while len(terms) > 1:
+        odd = terms[-1:] if len(terms) % 2 else []
+        terms = [p + q for p, q in zip(terms[0::2], terms[1::2])] + odd
+    return terms[0]
+
+
 def eliminate(a):
     n = a.shape[0]
-    ri = lax.broadcasted_iota(jnp.int32, (n, n), 0)
-    ci = lax.broadcasted_iota(jnp.int32, (n, n), 1)
-    for k in range(n):
-        row = a[k : k + 1, :]
-        m = jnp.where(ri[:, :1] > k, a[:, k : k + 1] * (1.0 / a[k : k + 1, k : k + 1]), 0.0)
-        rowz = jnp.where(ci[:1] == k, 1.0, row)
-        a = jnp.where((ci == k) & (ri > k), 0.0, a) - m * rowz
-    diagonal = jnp.sum(jnp.where(ri == ci, a, 0.0), axis=1, keepdims=True)
-    root = lax.rsqrt(diagonal)
-    upper = jnp.where(ri <= ci, a, 0.0) * root
-    inverse = (jnp.where(ri > ci, a, 0.0) + jnp.where(ri == ci, 1.0, 0.0)) * root
-    return upper, inverse
+    b = 8
+    rows = [a[b * i : b * i + b, :] for i in range(n // b)]
+    ci = lax.broadcasted_iota(jnp.int32, (b, n), 1)
+    ri = lax.broadcasted_iota(jnp.int32, (b, n), 0)
+    unit = [jnp.where(ri == j, 1.0, 0.0) for j in range(b)]
+
+    def lane(v, c):
+        return jnp.broadcast_to(v[:, c : c + 1], (b, n))
+
+    pivot = [lane(rows[0], j) for j in range(b)]
+    uppers, inverses = [], []
+    for p in range(n // b):
+        q = rows[p]
+        x = list(unit)
+        inside = (ci >= b * p) & (ci < b * p + b)
+        q1 = jnp.where(inside, jnp.where(ci - b * p == ri, 1.0, 0.0), q)
+        more = p + 1 < n // b
+        if more:
+            below = rows[p + 1]
+            below_old = [lane(below, b * p + j) for j in range(b)]
+            below_new = [lane(below, b * p + b + j) for j in range(b)]
+            ahead = [lane(q, b * p + b + j) for j in range(b)]
+        for k in range(b):
+            value = jnp.broadcast_to(pivot[k][k : k + 1, :], (b, n))
+            inv = 1.0 / value
+            root = lax.rsqrt(value)
+            col = jnp.where(ri == k, 0.0, pivot[k])
+            fac = jnp.where(ri == k, -1.0, pivot[k])
+            col_inv = col * inv
+            under = jnp.where(ri > k, col_inv, 0.0)
+            fresh = []
+            for j in range(b):
+                if j == k:
+                    fresh.append(jnp.where(ri == k, inv, -col_inv))
+                else:
+                    fresh.append(
+                        jnp.where(ri == k, 0.0, pivot[j]) - (fac * pivot[j][k : k + 1, :]) * inv
+                    )
+            pivot = fresh
+            gain = jnp.where(ri == k, root, 1.0)
+            for j in range(k + 1):
+                x[j] = (x[j] - under * x[j][k : k + 1, :]) * gain
+        z = tree([pivot[j] * q1[j : j + 1, :] for j in range(b)])
+        if more:
+            pivot_next = []
+            for c in range(b):
+                part = tree([pivot[j] * ahead[c][j : j + 1, :] for j in range(b)])
+                pivot_next.append(
+                    below_new[c] - tree([below_old[k] * part[k : k + 1, :] for k in range(b)])
+                )
+        z_rows = [jnp.broadcast_to(z[j : j + 1, :], (b, n)) for j in range(b)]
+        for i in range(p + 1, n // b):
+            src = rows[i]
+            rows[i] = jnp.where(inside, 0.0, src) - tree(
+                [lane(src, b * p + j) * z_rows[j] for j in range(b)]
+            )
+        upper = tree([x[j] * q[j : j + 1, :] for j in range(b)])
+        inverse = tree([x[j] * q1[j : j + 1, :] for j in range(b)])
+        diag = ci - b * p >= ri
+        uppers.append(jnp.where(diag, upper, 0.0))
+        inverses.append(jnp.where(ci - b * p <= ri, inverse, 0.0))
+        if more:
+            pivot = pivot_next
+    return jnp.concatenate(uppers, axis=0), jnp.concatenate(inverses, axis=0)
 
 
 def factor_kernel(scale, g_ref, t_hbm, o_hbm, r_ref, rows, w_ref, stage, in_sem, out_sem):
@@ -336,18 +405,21 @@
             at += 1
     r, w = {}, {}
     for p in range(n):
+        held = {}
+        for j in range(p):
+            held[j] = tree([exact(r[k, p], w[k, j], TN) for k in range(j, p)])
         r[p, p], w[p, p] = eliminate(g[p, p])
-        for j in range(p + 1, n):
-            r[p, j] = exact(w[p, p], g[p, j], NN)
+        if p + 1 < n:
+            ahead = exact(w[p, p], jnp.concatenate([g[p, j] for j in range(p + 1, n)], axis=1), NN)
+            for j in range(p + 1, n):
+                r[p, j] = ahead[:, (j - p - 1) * b : (j - p) * b]
         for i in range(p + 1, n):
             for j in range(i, n):
                 g[i, j] = g[i, j] - exact(r[p, i], r[p, j], TN)
-    for i in range(n):
-        for j in range(i):
-            total = exact(r[j, i], w[j, j], TN)
-            for k in range(j + 1, i):
-                total = total + exact(r[k, i], w[k, j], TN)
-            w[i, j] = -exact(w[i, i], total, NN)
+        if p:
+            behind = exact(w[p, p], jnp.concatenate([held[j] for j in range(p)], axis=1), NN)
+            for j in range(p):
+                w[p, j] = -behind[:, j * b : (j + 1) * b]
     for i in range(n):
         for j in range(n):
             spot = (slice(i * b, (i + 1) * b), slice(j * b, (j + 1) * b))
@@ -365,9 +437,19 @@
         if at >= 2:
             outs[at - 2].wait()
         part = rows[at * chunk : (at + 1) * chunk, :]
-        value = lax.dot_general(w_ref[0], part, NT, preferred_element_type=jnp.float32)
-        value += lax.dot_general(w_ref[1], part, NT, preferred_element_type=jnp.float32)
-        stage[slot] = value.astype(jnp.bfloat16)
+        for top, end in ((0, 256), (256, 512)):
+            value = tree(
+                [
+                    lax.dot_general(
+                        w_ref[k, top:end, :end],
+                        part[:, :end],
+                        NT,
+                        preferred_element_type=jnp.float32,
+                    )
+                    for k in range(2)
+                ]
+            )
+            stage[slot, top:end] = value.astype(jnp.bfloat16)
         outs.append(
             pltpu.make_async_copy(
                 stage.at[slot], o_hbm.at[:, pl.ds(at * chunk, chunk)], out_sem.at[slot]
@@ -447,40 +529,29 @@
     )(is_top, vt, vt, vt, west, east, south, north, lon_m, lat_m)
 
     dma = pltpu.SemaphoreType.DMA
-    total = pl.pallas_call(
+    total, picked = pl.pallas_call(
         sum_kernel,
-        in_specs=[VMEM],
-        out_specs=VMEM,
-        out_shape=shape((2, 16, 40, 128), f32),
+        in_specs=[SMEM, VMEM, ANY],
+        out_specs=[VMEM, ANY],
+        out_shape=[shape((2, 16, 40, 128), f32), shape((cells, cols), bf16)],
         scratch_shapes=[
+            pltpu.VMEM((cells, cols), bf16),
+            pltpu.VMEM((cells, 4, cols // 4), f32),
+            pltpu.VMEM((cells, 4, cols // 4), f32),
             pltpu.VMEM((16, 40, 128), f32),
             pltpu.VMEM((16, 40, 128), f32),
             pltpu.VMEM((16, 40, 128), f32),
             pltpu.VMEM((8, 40, 128), f32),
             pltpu.VMEM((2, 40, 128), f32),
             pltpu.VMEM((16, 40, 128), f32),
-            dma((1,)),
-            dma((1,)),
-            dma((15,)),
-            dma((15,)),
-            dma((7,)),
-            dma((7,)),
-            dma((15,)),
-            dma((15,)),
-            dma((1,)),
-            dma((1,)),
+            *[dma((n,)) for n in (1, 1, 15, 15, 7, 7, 15, 15, 1, 1)],
+            dma(()),
+            dma((4,)),
         ],
-        compiler_params=pltpu.CompilerParams(collective_id=1, has_side_effects=True),
-    )(gram.reshape(2, 16, 40, 128))
-
-    picked = pl.pallas_call(
-        pick_kernel,
-        in_specs=[SMEM, VMEM],
-        out_specs=VMEM,
-        out_shape=shape((cells, cols), bf16),
-        scratch_shapes=[pltpu.VMEM((cells, 4, 128), f32), pltpu.VMEM((cells, 4, 128), f32)],
-        compiler_params=params,
-    )(wet_index, f)
+        compiler_params=pltpu.CompilerParams(
+            collective_id=1, has_side_effects=True, vmem_limit_bytes=BIG
+        ),
+    )(wet_index, gram.reshape(2, 16, 40, 128), f)
 
     scale = math.sqrt(cells * n_lat * n_lon)
     basis, r_factor = pl.pallas_call(
@@ -491,7 +562,7 @@
         scratch_shapes=[
             pltpu.VMEM((cells, cols), bf16),
             pltpu.VMEM((2, cols, cols), bf16),
-            pltpu.VMEM((2, cols, 768), bf16),
+            pltpu.VMEM((2, cols, 1024), bf16),
             dma(()),
             dma((2,)),
         ],

time: 164 us -> 103 us (0.63)
  Pallas kernels: 161 us -> 100 us
    pallas_call x2 -> x1, Pallas kernels: 63.5 us -> 30.8 us  [shards(): pl.pallas_call(sum_kernel, in_specs=[SMEM, VMEM, ANY], out_specs=[VMEM, A...]
    pallas_call x1, Pallas kernels: 58.8 us -> 31 us  [shards(): pl.pallas_call(functools.partial(factor_kernel, scale), in_specs=[VMEM, A...]
where the time goes in v2:
time: 103 us
  Pallas kernels  100 us (97%)
  between operations  1.48 us (1%)
  local copies, waits for them, and re-layouts  1.36 us (1%)
    pallas_call x1, Pallas kernels, shards(): pl.pallas_call(functools.partial(factor_kernel, scale), in_specs=[VMEM, A...  31 us
    pallas_call x1, Pallas kernels, shards(): pl.pallas_call(sum_kernel, in_specs=[SMEM, VMEM, ANY], out_specs=[VMEM, A...  30.8 us
    pallas_call x1, Pallas kernels, shards(): pl.pallas_call(functools.partial(halo_kernel, n_lat, n_lon), in_specs=[AN...  15.7 us
    pallas_call x1, Pallas kernels, shards(): pl.pallas_call(field_kernel, grid=(nx // width,), in_specs=[SMEM, pl.Bloc...  10.4 us
    pallas_call x1, Pallas kernels, shards(): pl.pallas_call(turn_kernel, grid=(cols // lane,), in_specs=[pl.BlockSpec(...  10.2 us
    pallas_call x1, Pallas kernels, shards(): pl.pallas_call(metric_kernel, in_specs=[VMEM, SMEM, VMEM, VMEM], out_spec...  2.08 us

profile of v2, /device:TPU:1, one launch (start us, length us, event | category | flops | bytes accessed | tf_op | source)
XLA Modules:
  0.0 103.0 jit_solution(15965691706844918440)
XLA Ops:
  1.3 1.4 %reshape.24.idx_ref = s32[6,1024]{1,0:T(8,128)} reshape(s32[6144]{0:T(1024)} %idx.1) | data formatting | bytes 49152 | tf_op jit(solution)/shard_map/reshape | solution.py:477
  2.6 2.1 %shard_map.70 = (f32[48,128]{1,0:T(8,128)}, f32[48,128]{1,0:T(8,128)}) custom-call(s32[6,1024]{1,0:T(8,128)} %reshape.24.idx_ref, s32[1]{0:T(128)S(6)} %copy.7.count_ref, f32[48,128]{1,0:T(8,128)} %lon_ref.1, f32[48,128]{1,0:T(8,128)} %lat_ref.1), custom_call_target="tpu_custom_call" | custom-call | tf_op jit(solution)/shard_map/pallas_call | solution.py:471
  4.7 10.2 %shard_map.68 = (bf16[48,128,512]{2,1,0:T(8,128)(2,1)}, f32[48,512]{1,0:T(8,128)}, f32[48,512]{1,0:T(8,128)}) custom-call(bf16[512,48,128]{2,1,0:T(8,128)(2,1)} %bitcast.4), custom_call_target="tpu_custom_call" | custom-call | tf_op jit(solution)/shard_map/pallas_call | solution.py:480
  15.0 15.7 %shard_map.69 = (bf16[128,512]{1,0:T(8,128)(2,1)}, bf16[128,512]{1,0:T(8,128)(2,1)}, f32[48,512]{1,0:T(8,128)}, f32[48,512]{1,0:T(8,128)}) custom-call(bf16[48,128,512]{2,1,0:T(8,128)(2,1)} %get-tuple-element.15.vt.before.after, f32[48,512]{1,0:T(8,128)} %get-tuple-element.16.north_edge, f32[48,512]{1,0:T(8,128)} %get-tuple-element.17.south_edge), custom_call_target="tpu_custom_call" | custom-call | tf_op jit(solution)/shard_map/pallas_call | solution.py:494
  30.6 10.4 %shard_map.71 = (bf16[6144,512]{1,0:T(8,128)(2,1)}, f32[10,128,128]{2,1,0:T(8,128)}) custom-call(s32[1]{0:T(128)} %bitcast.top_ref, bf16[48,128,512]{2,1,0:T(8,128)(2,1)} %get-tuple-element.15.vt.before.after, bf16[48,128,512]{2,1,0:T(8,128)(2,1)} %get-tuple-element.15.vt.before.after, bf16[48,128,512]{2,1,0:T(8,128)(2,1)} %get-tuple-element.15.vt.before.after, ...), custom_call_target="tpu_custom_call" | custom-call | tf_op jit(solution)/shard_map/pallas_call | solution.py:507
  41.0 30.8 %shard_map.72 = (f32[2,16,40,128]{3,2,1,0:T(8,128)}, bf16[6144,512]{1,0:T(8,128)(2,1)}) custom-call(s32[6144]{0:T(1024)} %idx.1, f32[2,16,40,128]{3,2,1,0:T(8,128)} %bitcast.5, bf16[6144,512]{1,0:T(8,128)(2,1)} %get-tuple-element.25.f_hbm), custom_call_target="tpu_custom_call" | custom-call | tf_op jit(solution)/shard_map/pallas_call | solution.py:532
  71.8 31.0 %shard_map.73 = (bf16[512,6144]{1,0:T(8,128)(2,1)}, f32[512,512]{1,0:T(8,128)}) custom-call(f32[10,128,128]{2,1,0:T(8,128)} %bitcast.6, bf16[6144,512]{1,0:T(8,128)(2,1)} %get-tuple-element.27.t_hbm), custom_call_target="tpu_custom_call" | custom-call | tf_op jit(solution)/shard_map/pallas_call | solution.py:557

commit v3 on v2

v3 whole, which is shorter than its diff:
```python
import functools
import math

import jax
import jax.numpy as jnp
from jax import lax
from jax.experimental import pallas as pl
from jax.experimental.pallas import tpu as pltpu
from jax.sharding import PartitionSpec as P

MESH = pl.DeviceIdType.MESH
VMEM = pl.BlockSpec(memory_space=pltpu.VMEM)
SMEM = pl.BlockSpec(memory_space=pltpu.SMEM)
ANY = pl.BlockSpec(memory_space=pl.ANY)
BIG = 60 << 20
PIECE = 1536
NT = (((1,), (1,)), ((), ()))
TN = (((0,), (0,)), ((), ()))
NN = (((1,), (0,)), ((), ()))


def field_kernel(
    n_lat, n_lon, idx, count, lon_ref, lat_ref, v_hbm, f_hbm, gram_ref,
    vin, wide, vt, f, lon_t, lat_t, acc, edge, edge16, from16, south, north,
    load_sem, store_sem, send, recv,
):
    lat, lon = lax.axis_index("lat"), lax.axis_index("lon")
    nx, ny = lon_ref.shape
    lane = vin.shape[1]
    top = lat // (n_lat - 1)
    is_top = lat == n_lat - 1
    right = (lat, lax.rem(lon + 1, n_lon))
    left = (lat, lax.rem(lon + n_lon - 1, n_lon))
    up = (lat + 1 - top, lon + top * (n_lon - 1 - 2 * lon))
    down = (jnp.where(lat == 0, lat, lat - 1), lon)

    def load(step):
        c = lax.rem(step, 2) * 2 + step // 2
        return pltpu.make_async_copy(
            v_hbm.at[pl.ds(c * lane, lane)], vin.at[lax.rem(step, 2)], load_sem.at[lax.rem(step, 2)]
        )

    load(0).start()
    barrier = pltpu.get_barrier_semaphore()
    for other in (right, left, up):
        pl.semaphore_signal(barrier, inc=1, device_id=other, device_id_type=MESH)

    @pl.when(lat > 0)
    def _():
        pl.semaphore_signal(barrier, inc=1, device_id=down, device_id_type=MESH)

    live = count[0]
    total = jnp.zeros((nx, ny), jnp.float32)
    width = 8 * ny
    for at in range(nx // 8):
        cell = jnp.concatenate([idx[8 * at + i : 8 * at + i + 1, :] for i in range(8)], axis=1)
        place = lax.broadcasted_iota(jnp.int32, (1, width), 1) + at * width
        column = jnp.where(place < live, cell // ny, -1)
        hot_x = lax.broadcasted_iota(jnp.int32, (nx, width), 0) == column
        hot_y = lax.broadcasted_iota(jnp.int32, (ny, width), 0) == cell % ny
        total += lax.dot_general(
            hot_x.astype(jnp.float32).astype(jnp.bfloat16),
            hot_y.astype(jnp.float32).astype(jnp.bfloat16),
            NT,
            preferred_element_type=jnp.float32,
        )
    lon_m = 0.5 * lon_ref[...] * total
    lat_m = 0.5 * lat_ref[...] * total
    group = lon_t.shape[2]
    for at in range(nx // group):
        lon_t[at] = lon_m[at * group : (at + 1) * group].T
        lat_t[at] = lat_m[at * group : (at + 1) * group].T
    pl.semaphore_wait(barrier, jnp.where(lat > 0, 4, 3))

    def copy(src, dst, c, out, into, to):
        return pltpu.make_async_remote_copy(
            src_ref=src,
            dst_ref=dst,
            send_sem=send.at[c, out],
            recv_sem=recv.at[c, into],
            device_id=to,
            device_id_type=MESH,
        )

    def lanes(c):
        return pl.ds(pl.multiple_of(c * lane, lane), lane)

    def to_right(c):
        return copy(vt.at[nx, :, lanes(c)], vt.at[0, :, lanes(c)], c, 0, 0, right)

    def to_left(c):
        return copy(vt.at[1, :, lanes(c)], vt.at[nx + 1, :, lanes(c)], c, 1, 1, left)

    def to_up(c):
        return copy(edge16.at[1, c], from16.at[0, c], c, 2, 2, up)

    def to_fold(c):
        return copy(edge16.at[1, c], from16.at[1, c], c, 2, 3, up)

    def to_down(c):
        return copy(edge16.at[0, c], from16.at[1, c], c, 3, 3, down)

    def turn(step, _):
        c = lax.rem(step, 2) * 2 + step // 2
        load(step).wait()

        @pl.when(step < 3)
        def _():
            load(step + 1).start()

        wide[...] = vin[lax.rem(step, 2)].astype(jnp.float32)
        for x in range(nx):
            turned = wide[:, x, :].T
            vt[x + 1, :, lanes(c)] = turned.astype(jnp.bfloat16)
            edge[0, x : x + 1, :] = turned[:1, :]
            edge[1, x : x + 1, :] = turned[-1:, :]
        edge16[0, c] = edge[0].astype(jnp.bfloat16)
        edge16[1, c] = edge[1].astype(jnp.bfloat16)

        @pl.when(is_top)
        def _():
            to_fold(c).start()

        @pl.when(jnp.logical_not(is_top))
        def _():
            to_up(c).start()

        @pl.when(lat > 0)
        def _():
            to_down(c).start()

        to_right(c).start()
        to_left(c).start()
        return 0

    lax.fori_loop(0, 4, turn, 0)

    row = lax.broadcasted_iota(jnp.int32, (ny, 1), 0)
    iy = lax.broadcasted_iota(jnp.int32, (ny, ny), 0)
    ix = lax.broadcasted_iota(jnp.int32, (ny, ny), 1)
    band = (ix == iy + 1).astype(jnp.float32) - (ix == iy - 1).astype(jnp.float32)
    band = band.astype(jnp.bfloat16)
    acc[...] = jnp.zeros_like(acc)

    for h in range(2):
        for c in (h, 2 + h):
            to_right(c).wait_recv()
            to_left(c).wait_recv()
            to_fold(c).wait_recv()
            arrived = from16[1, c].astype(jnp.float32)
            north[c] = jnp.where(is_top, -arrived, arrived)

            @pl.when(lat == 0)
            def _():
                south[c] = jnp.zeros((nx, lane), jnp.float32)

            @pl.when(lat > 0)
            def _():
                to_up(c).wait_recv()
                south[c] = from16[0, c].astype(jnp.float32)

        cu, cv = h, 2 + h
        lu, lv = slice(cu * lane, cu * lane + lane), slice(cv * lane, cv * lane + lane)

        def fields(at_group, _):
            m_lon, m_lat = lon_t[at_group], lat_t[at_group]
            for at in range(group):
                x = at_group * group + at
                x_top = x + top * (nx - 1 - 2 * x)
                here = pl.ds(pl.multiple_of(x * ny, ny), ny)
                a, b = m_lon[:, at : at + 1], m_lat[:, at : at + 1]
                u_x = vt[x + 2, :, lu].astype(jnp.float32) - vt[x, :, lu].astype(jnp.float32)
                v_x = vt[x + 2, :, lv].astype(jnp.float32) - vt[x, :, lv].astype(jnp.float32)

                def over_y(c, where):
                    inner = lax.dot_general(
                        band, vt[x + 1, :, where], NN, preferred_element_type=jnp.float32
                    )
                    inner = inner + jnp.where(row == ny - 1, north[c, pl.ds(x_top, 1), :], 0.0)
                    return inner - jnp.where(row == 0, south[c, pl.ds(x, 1), :], 0.0)

                f[here, lu] = (a * v_x - b * over_y(cu, lu)).astype(jnp.bfloat16)
                f[here, lv] = (a * u_x + b * over_y(cv, lv)).astype(jnp.bfloat16)
            if h == 1:
                span = pl.ds(pl.multiple_of(at_group * (group * ny), group * ny), group * ny)
                pltpu.make_async_copy(f.at[span], f_hbm.at[span], store_sem.at[at_group]).start()
                acc[...] += lax.dot_general(
                    f[span, :], f[span, :], TN, preferred_element_type=jnp.float32
                )
            return 0

        lax.fori_loop(0, nx // group, fields, 0)
    at = 0
    for i in range(4):
        for j in range(i, 4):
            gram_ref[at] = acc[i * 128 : (i + 1) * 128, j * 128 : (j + 1) * 128]
            at += 1
    for at in range(nx // group):
        span = pl.ds(at * group * ny, group * ny)
        pltpu.make_async_copy(f.at[span], f_hbm.at[span], store_sem.at[at]).wait()
    for c in range(4):
        to_right(c).wait_send()
        to_left(c).wait_send()

        @pl.when(is_top)
        def _():
            to_fold(c).wait_send()

        @pl.when(jnp.logical_not(is_top))
        def _():
            to_up(c).wait_send()

        @pl.when(lat > 0)
        def _():
            to_down(c).wait_send()


def sum_kernel(
    idx, g, f_hbm, out, t_hbm, rows, spread, picked, r0, s0, r1, r2, s1, r3,
    send0, recv0, send1, recv1, send2, recv2, send3, recv3, send4, recv4, load_sem, store_sem,
):
    lat, lon = lax.axis_index("lat"), lax.axis_index("lon")
    core, cx = lax.rem(lat, 2), lat // 2
    cy, cz = lon // 8, lax.rem(lon, 8)
    mine = cx * 4 + cy
    mate = (lat + 1 - 2 * core, lon)
    cells, cols = rows.shape
    piece = cells // 4

    def plane(off):
        spot = lax.rem(mine + off, 16)
        return spot, (2 * (spot // 4) + core, 8 * lax.rem(spot, 4) + cz)

    def column(off):
        return (lat, 8 * cy + lax.rem(cz + off, 8))

    def widen(at, _):
        here = pl.ds(pl.multiple_of(at * 128, 128), 128)
        spread[here] = rows[here, :].astype(jnp.float32).reshape(128, 4, cols // 4)
        return 0

    def pick(at, _):
        base = at * 64
        taken = [spread[idx[base + u]] for u in range(64)]
        for u in range(64):
            picked[base + u] = taken[u]
        return 0

    def narrow(at, _):
        here = pl.ds(pl.multiple_of(at * 128, 128), 128)
        rows[here, :] = picked[here].reshape(128, cols).astype(jnp.bfloat16)
        return 0

    def pick_piece(at):
        lax.fori_loop(at * piece // 64, (at + 1) * piece // 64, pick, 0)

    def store_piece(at):
        lax.fori_loop(at * piece // 128, (at + 1) * piece // 128, narrow, 0)
        here = pl.ds(at * piece, piece)
        item = pltpu.make_async_copy(rows.at[here], t_hbm.at[here], store_sem.at[at])
        item.start()
        return item

    load = pltpu.make_async_copy(f_hbm, rows, load_sem)
    load.start()
    barrier = pltpu.get_barrier_semaphore()
    pl.semaphore_signal(barrier, inc=1, device_id=mate, device_id_type=MESH)
    for off in range(1, 16):
        pl.semaphore_signal(barrier, inc=1, device_id=plane(off)[1], device_id_type=MESH)
    for off in range(1, 8):
        pl.semaphore_signal(barrier, inc=1, device_id=column(off), device_id_type=MESH)
    pl.semaphore_wait(barrier, 23)

    def copy(src, dst, send, recv, to):
        return pltpu.make_async_remote_copy(
            src_ref=src, dst_ref=dst, send_sem=send, recv_sem=recv, device_id=to, device_id_type=MESH
        )

    first = copy(g.at[1 - core], r0, send0.at[0], recv0.at[0], mate)
    first.start()
    first.wait_recv()
    s0[...] = g[core] + r0[...]
    second = []
    for off in range(1, 16):
        spot, to = plane(off)
        second.append(copy(s0.at[spot], r1.at[mine], send1.at[off - 1], recv1.at[off - 1], to))
        second[-1].start()
    r1[mine] = s0[mine]
    load.wait()
    lax.fori_loop(0, cells // 128, widen, 0)
    pick_piece(0)
    for item in second:
        item.wait_recv()
    total = r1[0]
    for at in range(1, 16):
        total = total + r1[at]
    s1[0] = total
    r2[cz] = total
    third = []
    for off in range(1, 8):
        third.append(copy(s1.at[0], r2.at[cz], send2.at[off - 1], recv2.at[off - 1], column(off)))
        third[-1].start()
    pick_piece(1)
    pick_piece(2)
    for item in third:
        item.wait_recv()
    total = r2[0]
    for at in range(1, 8):
        total = total + r2[at]
    s1[1] = total
    r3[mine] = total
    fourth = []
    for off in range(1, 16):
        fourth.append(
            copy(s1.at[1], r3.at[mine], send3.at[off - 1], recv3.at[off - 1], plane(off)[1])
        )
        fourth[-1].start()
    pick_piece(3)
    stores = [store_piece(at) for at in range(4)]
    for item in fourth:
        item.wait_recv()
    last = copy(r3, out.at[core], send4.at[0], recv4.at[0], mate)
    last.start()
    out[core] = r3[...]
    last.wait_recv()
    for item in stores:
        item.wait()
    for item in [first, *second, *third, *fourth, last]:
        item.wait_send()


def exact(a, b, dims):
    return lax.dot_general(
        a, b, dims, precision=lax.Precision.HIGHEST, preferred_element_type=jnp.float32
    )


def tree(terms):
    while len(terms) > 1:
        odd = terms[-1:] if len(terms) % 2 else []
        terms = [p + q for p, q in zip(terms[0::2], terms[1::2])] + odd
    return terms[0]


def eliminate(a, beside):
    n = a.shape[0]
    b = 8
    rows = [a[b * i : b * i + b, :] for i in range(n // b)]
    ci = lax.broadcasted_iota(jnp.int32, (b, n), 1)
    ri = lax.broadcasted_iota(jnp.int32, (b, n), 0)
    unit = [jnp.where(ri == j, 1.0, 0.0) for j in range(b)]

    def lane(v, c):
        return jnp.broadcast_to(v[:, c : c + 1], (b, n))

    pivot = [lane(rows[0], j) for j in range(b)]
    uppers, inverses = [], []
    for p in range(n // b):
        q = rows[p]
        x = list(unit)
        inside = (ci >= b * p) & (ci < b * p + b)
        q1 = jnp.where(inside, jnp.where(ci - b * p == ri, 1.0, 0.0), q)
        more = p + 1 < n // b
        if more:
            below = rows[p + 1]
            below_old = [lane(below, b * p + j) for j in range(b)]
            below_new = [lane(below, b * p + b + j) for j in range(b)]
            ahead = [lane(q, b * p + b + j) for j in range(b)]
        for k in range(b):
            value = jnp.broadcast_to(pivot[k][k : k + 1, :], (b, n))
            inv = 1.0 / value
            root = lax.rsqrt(value)
            col = jnp.where(ri == k, 0.0, pivot[k])
            fac = jnp.where(ri == k, -1.0, pivot[k])
            col_inv = col * inv
            under = jnp.where(ri > k, col_inv, 0.0)
            fresh = []
            for j in range(b):
                if j == k:
                    fresh.append(jnp.where(ri == k, inv, -col_inv))
                else:
                    fresh.append(
                        jnp.where(ri == k, 0.0, pivot[j]) - (fac * pivot[j][k : k + 1, :]) * inv
                    )
            pivot = fresh
            gain = jnp.where(ri == k, root, 1.0)
            for j in range(k + 1):
                x[j] = (x[j] - under * x[j][k : k + 1, :]) * gain
        z = tree([pivot[j] * q1[j : j + 1, :] for j in range(b)])
        if more:
            pivot_next = []
            for c in range(b):
                part = tree([pivot[j] * ahead[c][j : j + 1, :] for j in range(b)])
                pivot_next.append(
                    below_new[c] - tree([below_old[k] * part[k : k + 1, :] for k in range(b)])
                )
        z_rows = [jnp.broadcast_to(z[j : j + 1, :], (b, n)) for j in range(b)]
        for i in range(p + 1, n // b):
            src = rows[i]
            rows[i] = jnp.where(inside, 0.0, src) - tree(
                [lane(src, b * p + j) * z_rows[j] for j in range(b)]
            )
        upper = tree([x[j] * q[j : j + 1, :] for j in range(b)])
        inverse = tree([x[j] * q1[j : j + 1, :] for j in range(b)])
        diag = ci - b * p >= ri
        uppers.append(jnp.where(diag, upper, 0.0))
        inverses.append(jnp.where(ci - b * p <= ri, inverse, 0.0))
        if more:
            pivot = pivot_next
        for _ in range(-(-len(beside) // (n // b - p))):
            beside.pop(0)()
    return jnp.concatenate(uppers, axis=0), jnp.concatenate(inverses, axis=0)


def factor_kernel(scale, g_ref, t_hbm, o_hbm, r_ref, rows, w_ref, stage, in_sem, out_sem):
    load = pltpu.make_async_copy(t_hbm, rows, in_sem)
    load.start()
    b, n = 128, 4
    chunk = PIECE
    pieces = rows.shape[0] // chunk
    g, r, w, held, outs = {}, {}, {}, {}, []
    at = 0
    for i in range(n):
        for j in range(i, n):
            g[i, j] = g_ref[at]
            at += 1

    def spot(i, j):
        return slice(i * b, (i + 1) * b), slice(j * b, (j + 1) * b)

    def row_of(p, j):
        r[p, j] = exact(w[p, p], g[p, j], NN)

    def update(p, i, j):
        g[i, j] = g[i, j] - exact(r[p, i], r[p, j], TN)

    def hold(i, j):
        held[i, j] = tree([exact(r[k, i], w[k, j], TN) for k in range(j, i)])

    def store_w(i, j):
        value = w[i, j] * scale
        high = value.astype(jnp.bfloat16)
        low = (value - high.astype(jnp.float32)).astype(jnp.bfloat16)
        w_ref[2 * i * b : (2 * i + 1) * b, spot(i, j)[1]] = high
        w_ref[(2 * i + 1) * b : (2 * i + 2) * b, spot(i, j)[1]] = low

    def finish_row(p):
        if p:
            behind = exact(w[p, p], jnp.concatenate([held[p, j] for j in range(p)], axis=1), NN)
            for j in range(p):
                w[p, j] = -behind[:, j * b : (j + 1) * b]
        for j in range(p + 1):
            store_w(p, j)

    def store_r(p):
        for j in range(n):
            r_ref[spot(p, j)] = r[p, j] * (1.0 / scale) if j >= p else jnp.zeros((b, b), jnp.float32)

    def basis_piece(p, at):
        end = (p + 1) * b
        here = slice(at * chunk, (at + 1) * chunk)
        both = lax.dot_general(
            w_ref[2 * p * b : (2 * p + 2) * b, :end],
            rows[here, :end],
            NT,
            preferred_element_type=jnp.float32,
        )
        stage[p, :, here] = (both[:b] + both[b:]).astype(jnp.bfloat16)

    def send_row(p):
        item = pltpu.make_async_copy(stage.at[p], o_hbm.at[pl.ds(p * b, b), :], out_sem.at[p])
        item.start()
        outs.append(item)

    beside = []
    for p in range(n):
        r[p, p], w[p, p] = eliminate(g[p, p], beside)
        assert not beside
        if p == 0:
            load.wait()
        else:
            send_row(p - 1)
        if p + 1 < n:
            row_of(p, p + 1)
            update(p, p + 1, p + 1)
            for j in range(p + 2, n):
                beside.append(functools.partial(row_of, p, j))
                for i in range(p + 1, j + 1):
                    beside.append(functools.partial(update, p, i, j))
            beside.append(functools.partial(finish_row, p))
            for j in range(p + 1):
                beside.append(functools.partial(hold, p + 1, j))
            beside.append(functools.partial(store_r, p))
            for at in range(pieces):
                beside.append(functools.partial(basis_piece, p, at))
        else:
            finish_row(p)
            store_r(p)
            for at in range(pieces):
                basis_piece(p, at)
            send_row(p)
    for item in outs:
        item.wait()


def shards(n_lat, n_lon, velocity, lon_metric, lat_metric, wet_index, wet_count):
    days, nx, ny = velocity.shape[1:]
    cols = 2 * days
    cells = nx * ny
    f32, bf16 = jnp.float32, jnp.bfloat16
    shape = jax.ShapeDtypeStruct
    params = pltpu.CompilerParams(vmem_limit_bytes=BIG)

    dma = pltpu.SemaphoreType.DMA
    lane, group = 128, 16
    f, gram = pl.pallas_call(
        functools.partial(field_kernel, n_lat, n_lon),
        in_specs=[VMEM, SMEM, VMEM, VMEM, ANY],
        out_specs=[ANY, VMEM],
        out_shape=[shape((cells, cols), bf16), shape((10, 128, 128), f32)],
        scratch_shapes=[
            pltpu.VMEM((2, lane, nx, ny), bf16),
            pltpu.VMEM((lane, nx, ny), f32),
            pltpu.VMEM((nx + 2, ny, cols), bf16),
            pltpu.VMEM((cells, cols), bf16),
            pltpu.VMEM((nx // group, ny, group), f32),
            pltpu.VMEM((nx // group, ny, group), f32),
            pltpu.VMEM((cols, cols), f32),
            pltpu.VMEM((2, nx, lane), f32),
            pltpu.VMEM((2, 4, nx, lane), bf16),
            pltpu.VMEM((2, 4, nx, lane), bf16),
            pltpu.VMEM((4, nx, lane), f32),
            pltpu.VMEM((4, nx, lane), f32),
            dma((2,)),
            dma((3,)),
            dma((4, 4)),
            dma((4, 4)),
        ],
        compiler_params=pltpu.CompilerParams(
            collective_id=0, has_side_effects=True, vmem_limit_bytes=BIG
        ),
    )(
        wet_index.reshape(nx, ny), wet_count, lon_metric, lat_metric, velocity.reshape(cols, nx, ny)
    )

    total, picked = pl.pallas_call(
        sum_kernel,
        in_specs=[SMEM, VMEM, ANY],
        out_specs=[VMEM, ANY],
        out_shape=[shape((2, 16, 40, 128), f32), shape((cells, cols), bf16)],
        scratch_shapes=[
            pltpu.VMEM((cells, cols), bf16),
            pltpu.VMEM((cells, 4, cols // 4), f32),
            pltpu.VMEM((cells, 4, cols // 4), f32),
            pltpu.VMEM((16, 40, 128), f32),
            pltpu.VMEM((16, 40, 128), f32),
            pltpu.VMEM((16, 40, 128), f32),
            pltpu.VMEM((8, 40, 128), f32),
            pltpu.VMEM((2, 40, 128), f32),
            pltpu.VMEM((16, 40, 128), f32),
            *[dma((n,)) for n in (1, 1, 15, 15, 7, 7, 15, 15, 1, 1)],
            dma(()),
            dma((4,)),
        ],
        compiler_params=pltpu.CompilerParams(
            collective_id=1, has_side_effects=True, vmem_limit_bytes=BIG
        ),
    )(wet_index, gram.reshape(2, 16, 40, 128), f)

    scale = math.sqrt(cells * n_lat * n_lon)
    basis, r_factor = pl.pallas_call(
        functools.partial(factor_kernel, scale),
        in_specs=[VMEM, ANY],
        out_specs=[ANY, VMEM],
        out_shape=[shape((cols, cells), bf16), shape((cols, cols), f32)],
        scratch_shapes=[
            pltpu.VMEM((cells, cols), bf16),
            pltpu.VMEM((2 * cols, cols), bf16),
            pltpu.VMEM((4, 128, cells), bf16),
            dma(()),
            dma((4,)),
        ],
        compiler_params=params,
    )(total.reshape(10, 128, 128), picked)
    return basis, r_factor


def solution(mesh):
    n_lat, n_lon = mesh.shape["lat"], mesh.shape["lon"]
    placed = (
        P(None, None, "lon", "lat"),
        P("lon", "lat"),
        P("lon", "lat"),
        P(("lat", "lon")),
        P(("lat", "lon")),
    )
    return jax.shard_map(
        functools.partial(shards, n_lat, n_lon),
        mesh=mesh,
        in_specs=placed,
        out_specs=(P(None, ("lat", "lon")), P()),
        check_vma=False,
    )
```

time: 103 us -> 88.9 us (0.86)
  Pallas kernels: 100 us -> 87.2 us
  local copies, waits for them, and re-layouts: 1.36 us -> 0 us
    pallas_call x4 -> x1, Pallas kernels: 38.4 us -> 29.3 us  [shards(): pl.pallas_call(functools.partial(field_kernel, n_lat, n_lon), in_specs=[V...]
    pallas_call x1, Pallas kernels: 31 us -> 28.7 us  [shards(): pl.pallas_call(functools.partial(factor_kernel, scale), in_specs=[VMEM, A...]
    pallas_call x1, Pallas kernels: 30.8 us -> 29.2 us  [shards(): pl.pallas_call(sum_kernel, in_specs=[SMEM, VMEM, ANY], out_specs=[VMEM, A...]
    reshape x1 -> x0, local copies, waits for them, and re-layouts: 1.36 us -> none  [shards(): wet_index.reshape(6, -1)]
where the time goes in v3:
time: 88.9 us; the launch traced here: 88.6 us
  Pallas kernels  87.2 us (98%)
  between operations  1.47 us (2%)
    pallas_call x1, Pallas kernels, shards(): pl.pallas_call(functools.partial(field_kernel, n_lat, n_lon), in_specs=[V...  29.3 us
    pallas_call x1, Pallas kernels, shards(): pl.pallas_call(sum_kernel, in_specs=[SMEM, VMEM, ANY], out_specs=[VMEM, A...  29.2 us
    pallas_call x1, Pallas kernels, shards(): pl.pallas_call(functools.partial(factor_kernel, scale), in_specs=[VMEM, A...  28.7 us

profile of v3, /device:TPU:1, one launch (start us, length us, event | category | flops | bytes accessed | tf_op | source)
XLA Modules:
  0.0 88.6 jit_solution(2845408620557861521)
XLA Ops:
  1.3 29.3 %shard_map.68 = (bf16[6144,512]{1,0:T(8,128)(2,1)}, f32[10,128,128]{2,1,0:T(8,128)}) custom-call(s32[48,128]{1,0:T(8,128)} %bitcast.7, s32[1]{0:T(128)S(6)} %copy.7.count, f32[48,128]{1,0:T(8,128)} %lon_ref.1, f32[48,128]{1,0:T(8,128)} %lat_ref.1, bf16[512,48,128]{2,1,0:T(8,128)(2,1)} %bitcast.4), custom_call_target="tpu_custom_call" | custom-call | tf_op jit(solution)/shard_map/pallas_call | solution.py:516
  30.6 29.2 %shard_map.69 = (f32[2,16,40,128]{3,2,1,0:T(8,128)}, bf16[6144,512]{1,0:T(8,128)(2,1)}) custom-call(s32[6144]{0:T(1024)} %idx.1, f32[2,16,40,128]{3,2,1,0:T(8,128)} %bitcast.6, bf16[6144,512]{1,0:T(8,128)(2,1)} %get-tuple-element.7.f_hbm), custom_call_target="tpu_custom_call" | custom-call | tf_op jit(solution)/shard_map/pallas_call | solution.py:546
  59.8 28.7 %shard_map.70 = (bf16[512,6144]{1,0:T(8,128)(2,1)}, f32[512,512]{1,0:T(8,128)}) custom-call(f32[10,128,128]{2,1,0:T(8,128)} %bitcast.5, bf16[6144,512]{1,0:T(8,128)(2,1)} %get-tuple-element.9.t_hbm), custom_call_target="tpu_custom_call" | custom-call | tf_op jit(solution)/shard_map/pallas_call | solution.py:571

commit v4 on v3

--- a/solution.py
+++ b/solution.py
@@ -20,9 +20,11 @@
 
 
 def field_kernel(
-    n_lat, n_lon, idx, count, lon_ref, lat_ref, v_hbm, f_hbm, gram_ref,
+    n_lat, n_lon, order, idx, count, lon_ref, lat_ref, v_hbm, out, t_hbm,
     vin, wide, vt, f, lon_t, lat_t, acc, edge, edge16, from16, south, north,
+    spread, picked, g, r0, s0, r1, r2, s1, r3,
     load_sem, store_sem, send, recv,
+    send0, recv0, send1, recv1, send2, recv2, send3, recv3, send4, recv4,
 ):
     lat, lon = lax.axis_index("lat"), lax.axis_index("lon")
     nx, ny = lon_ref.shape
@@ -40,9 +42,23 @@
             v_hbm.at[pl.ds(c * lane, lane)], vin.at[lax.rem(step, 2)], load_sem.at[lax.rem(step, 2)]
         )
 
+    core, cx = lax.rem(lat, 2), lat // 2
+    cy, cz = lon // 8, lax.rem(lon, 8)
+    mine = cx * 4 + cy
+    mate = (lat + 1 - 2 * core, lon)
+
+    def plane(off):
+        spot = lax.rem(mine + off, 16)
+        return spot, (2 * (spot // 4) + core, 8 * lax.rem(spot, 4) + cz)
+
+    def along_z(off):
+        return (lat, 8 * cy + lax.rem(cz + off, 8))
+
     load(0).start()
     barrier = pltpu.get_barrier_semaphore()
-    for other in (right, left, up):
+    others = [right, left, up, mate]
+    others += [plane(off)[1] for off in range(1, 16)] + [along_z(off) for off in range(1, 8)]
+    for other in others:
         pl.semaphore_signal(barrier, inc=1, device_id=other, device_id_type=MESH)
 
     @pl.when(lat > 0)
@@ -70,7 +86,7 @@
     for at in range(nx // group):
         lon_t[at] = lon_m[at * group : (at + 1) * group].T
         lat_t[at] = lat_m[at * group : (at + 1) * group].T
-    pl.semaphore_wait(barrier, jnp.where(lat > 0, 4, 3))
+    pl.semaphore_wait(barrier, jnp.where(lat > 0, 27, 26))
 
     def copy(src, dst, c, out, into, to):
         return pltpu.make_async_remote_copy(
@@ -183,21 +199,149 @@
                 f[here, lv] = (a * u_x + b * over_y(cv, lv)).astype(jnp.bfloat16)
             if h == 1:
                 span = pl.ds(pl.multiple_of(at_group * (group * ny), group * ny), group * ny)
-                pltpu.make_async_copy(f.at[span], f_hbm.at[span], store_sem.at[at_group]).start()
                 acc[...] += lax.dot_general(
                     f[span, :], f[span, :], TN, preferred_element_type=jnp.float32
                 )
             return 0
 
         lax.fori_loop(0, nx // group, fields, 0)
-    at = 0
+    tile = 0
     for i in range(4):
         for j in range(i, 4):
-            gram_ref[at] = acc[i * 128 : (i + 1) * 128, j * 128 : (j + 1) * 128]
-            at += 1
-    for at in range(nx // group):
-        span = pl.ds(at * group * ny, group * ny)
-        pltpu.make_async_copy(f.at[span], f_hbm.at[span], store_sem.at[at]).wait()
+            for k in range(16):
+                half, spot, low = tile // 80, tile % 80 // 5, tile % 5 * 8
+                g[half, spot, low : low + 8, :] = acc[
+                    i * 128 + k * 8 : i * 128 + k * 8 + 8, j * 128 : (j + 1) * 128
+                ]
+                tile += 1
+    cells, cols = f.shape
+    spans = (pl.ds(0, 24), pl.ds(24, 16))
+    started = []
+
+    def widen(at, _):
+        here = pl.ds(pl.multiple_of(at * 128, 128), 128)
+        spread[here] = f[here, :].astype(jnp.float32).reshape(128, 4, cols // 4)
+        return 0
+
+    def pick(at, _):
+        base = at * 64
+        taken = [spread[order[base + u]] for u in range(64)]
+        for u in range(64):
+            picked[base + u] = taken[u]
+        return 0
+
+    def pick_part(low, high):
+        lax.fori_loop(low * 8, high * 8, pick, 0)
+
+    def narrow(at, _):
+        here = pl.ds(pl.multiple_of(at * 128, 128), 128)
+        f[here, :] = picked[here].reshape(128, cols).astype(jnp.bfloat16)
+        return 0
+
+    def go(src, dst, out_sem, in_sem, to):
+        item = pltpu.make_async_remote_copy(
+            src_ref=src,
+            dst_ref=dst,
+            send_sem=out_sem,
+            recv_sem=in_sem,
+            device_id=to,
+            device_id_type=MESH,
+        )
+        item.start()
+        started.append(item)
+        return item
+
+    def pair_start(k):
+        span = spans[k]
+        return go(g.at[1 - core, :, span], r0.at[:, span], send0.at[k], recv0.at[k], mate)
+
+    def gather_start(k, item):
+        span = spans[k]
+        item.wait_recv()
+        s0[:, span] = g[core, :, span] + r0[:, span]
+        items = []
+        for off in range(1, 16):
+            spot, to = plane(off)
+            items.append(
+                go(
+                    s0.at[spot, span],
+                    r1.at[mine, span],
+                    send1.at[k, off - 1],
+                    recv1.at[k, off - 1],
+                    to,
+                )
+            )
+        r1[mine, span] = s0[mine, span]
+        return items
+
+    def column_start(k, items):
+        span = spans[k]
+        for item in items:
+            item.wait_recv()
+        total = r1[0, span]
+        for at in range(1, 16):
+            total = total + r1[at, span]
+        s1[0, span] = total
+        r2[cz, span] = total
+        return [
+            go(
+                s1.at[0, span],
+                r2.at[cz, span],
+                send2.at[k, off - 1],
+                recv2.at[k, off - 1],
+                along_z(off),
+            )
+            for off in range(1, 8)
+        ]
+
+    def back_start(k, items):
+        span = spans[k]
+        for item in items:
+            item.wait_recv()
+        total = r2[0, span]
+        for at in range(1, 8):
+            total = total + r2[at, span]
+        s1[1, span] = total
+        r3[mine, span] = total
+        return [
+            go(
+                s1.at[1, span],
+                r3.at[mine, span],
+                send3.at[k, off - 1],
+                recv3.at[k, off - 1],
+                plane(off)[1],
+            )
+            for off in range(1, 16)
+        ]
+
+    def last_start(k, items):
+        span = spans[k]
+        for item in items:
+            item.wait_recv()
+        return go(r3.at[:, span], out.at[core, :, span], send4.at[k], recv4.at[k], mate)
+
+    pairs = [pair_start(k) for k in range(2)]
+    lax.fori_loop(0, cells // 128, widen, 0)
+    planes = [gather_start(k, pairs[k]) for k in range(2)]
+    pick_part(0, 4)
+    first = column_start(0, planes[0])
+    pick_part(4, 5)
+    columns = [first, column_start(1, planes[1])]
+    pick_part(5, 8)
+    first = back_start(0, columns[0])
+    pick_part(8, 9)
+    backs = [first, back_start(1, columns[1])]
+    pick_part(9, 12)
+    lax.fori_loop(0, cells // 128, narrow, 0)
+    store = pltpu.make_async_copy(f, t_hbm, store_sem)
+    store.start()
+    lasts = [last_start(k, backs[k]) for k in range(2)]
+    out[core] = r3[...]
+    for item in lasts:
+        item.wait_recv()
+    store.wait()
+    for item in started:
+        item.wait_send()
     for c in range(4):
         to_right(c).wait_send()
         to_left(c).wait_send()
@@ -213,120 +357,6 @@
         @pl.when(lat > 0)
         def _():
             to_down(c).wait_send()
-
-
-def sum_kernel(
-    idx, g, f_hbm, out, t_hbm, rows, spread, picked, r0, s0, r1, r2, s1, r3,
-    send0, recv0, send1, recv1, send2, recv2, send3, recv3, send4, recv4, load_sem, store_sem,
-):
-    lat, lon = lax.axis_index("lat"), lax.axis_index("lon")
-    core, cx = lax.rem(lat, 2), lat // 2
-    cy, cz = lon // 8, lax.rem(lon, 8)
-    mine = cx * 4 + cy
-    mate = (lat + 1 - 2 * core, lon)
-    cells, cols = rows.shape
-    piece = cells // 4
-
-    def plane(off):
-        spot = lax.rem(mine + off, 16)
-        return spot, (2 * (spot // 4) + core, 8 * lax.rem(spot, 4) + cz)
-
-    def column(off):
-        return (lat, 8 * cy + lax.rem(cz + off, 8))
-
-    def widen(at, _):
-        here = pl.ds(pl.multiple_of(at * 128, 128), 128)
-        spread[here] = rows[here, :].astype(jnp.float32).reshape(128, 4, cols // 4)
-        return 0
-
-    def pick(at, _):
-        base = at * 64
-        taken = [spread[idx[base + u]] for u in range(64)]
-        for u in range(64):
-            picked[base + u] = taken[u]
-        return 0
-
-    def narrow(at, _):
-        here = pl.ds(pl.multiple_of(at * 128, 128), 128)
-        rows[here, :] = picked[here].reshape(128, cols).astype(jnp.bfloat16)
-        return 0
-
-    def pick_piece(at):
-        lax.fori_loop(at * piece // 64, (at + 1) * piece // 64, pick, 0)
-
-    def store_piece(at):
-        lax.fori_loop(at * piece // 128, (at + 1) * piece // 128, narrow, 0)
-        here = pl.ds(at * piece, piece)
-        item = pltpu.make_async_copy(rows.at[here], t_hbm.at[here], store_sem.at[at])
-        item.start()
-        return item
-
-    load = pltpu.make_async_copy(f_hbm, rows, load_sem)
-    load.start()
-    barrier = pltpu.get_barrier_semaphore()
-    pl.semaphore_signal(barrier, inc=1, device_id=mate, device_id_type=MESH)
-    for off in range(1, 16):
-        pl.semaphore_signal(barrier, inc=1, device_id=plane(off)[1], device_id_type=MESH)
-    for off in range(1, 8):
-        pl.semaphore_signal(barrier, inc=1, device_id=column(off), device_id_type=MESH)
-    pl.semaphore_wait(barrier, 23)
-
-    def copy(src, dst, send, recv, to):
-        return pltpu.make_async_remote_copy(
-            src_ref=src, dst_ref=dst, send_sem=send, recv_sem=recv, device_id=to, device_id_type=MESH
-        )
-
-    first = copy(g.at[1 - core], r0, send0.at[0], recv0.at[0], mate)
-    first.start()
-    first.wait_recv()
-    s0[...] = g[core] + r0[...]
-    second = []
-    for off in range(1, 16):
-        spot, to = plane(off)
-        second.append(copy(s0.at[spot], r1.at[mine], send1.at[off - 1], recv1.at[off - 1], to))
-        second[-1].start()
-    r1[mine] = s0[mine]
-    load.wait()
-    lax.fori_loop(0, cells // 128, widen, 0)
-    pick_piece(0)
-    for item in second:
-        item.wait_recv()
-    total = r1[0]
-    for at in range(1, 16):
-        total = total + r1[at]
-    s1[0] = total
-    r2[cz] = total
-    third = []
-    for off in range(1, 8):
-        third.append(copy(s1.at[0], r2.at[cz], send2.at[off - 1], recv2.at[off - 1], column(off)))
-        third[-1].start()
-    pick_piece(1)
-    pick_piece(2)
-    for item in third:
-        item.wait_recv()
-    total = r2[0]
-    for at in range(1, 8):
-        total = total + r2[at]
-    s1[1] = total
-    r3[mine] = total
-    fourth = []
-    for off in range(1, 16):
-        fourth.append(
-            copy(s1.at[1], r3.at[mine], send3.at[off - 1], recv3.at[off - 1], plane(off)[1])
-        )
-        fourth[-1].start()
-    pick_piece(3)
-    stores = [store_piece(at) for at in range(4)]
-    for item in fourth:
-        item.wait_recv()
-    last = copy(r3, out.at[core], send4.at[0], recv4.at[0], mate)
-    last.start()
-    out[core] = r3[...]
-    last.wait_recv()
-    for item in stores:
-        item.wait()
-    for item in [first, *second, *third, *fourth, last]:
-        item.wait_send()
 
 
 def exact(a, b, dims):
@@ -513,11 +543,11 @@
 
     dma = pltpu.SemaphoreType.DMA
     lane, group = 128, 16
-    f, gram = pl.pallas_call(
+    total, picked = pl.pallas_call(
         functools.partial(field_kernel, n_lat, n_lon),
-        in_specs=[VMEM, SMEM, VMEM, VMEM, ANY],
-        out_specs=[ANY, VMEM],
-        out_shape=[shape((cells, cols), bf16), shape((10, 128, 128), f32)],
+        in_specs=[SMEM, VMEM, SMEM, VMEM, VMEM, ANY],
+        out_specs=[VMEM, ANY],
+        out_shape=[shape((2, 16, 40, 128), f32), shape((cells, cols), bf16)],
         scratch_shapes=[
             pltpu.VMEM((2, lane, nx, ny), bf16),
             pltpu.VMEM((lane, nx, ny), f32),
@@ -531,41 +561,32 @@
             pltpu.VMEM((2, 4, nx, lane), bf16),
             pltpu.VMEM((4, nx, lane), f32),
             pltpu.VMEM((4, nx, lane), f32),
-            dma((2,)),
-            dma((3,)),
-            dma((4, 4)),
-            dma((4, 4)),
-        ],
-        compiler_params=pltpu.CompilerParams(
-            collective_id=0, has_side_effects=True, vmem_limit_bytes=BIG
-        ),
-    )(
-        wet_index.reshape(nx, ny), wet_count, lon_metric, lat_metric, velocity.reshape(cols, nx, ny)
-    )
-
-    total, picked = pl.pallas_call(
-        sum_kernel,
-        in_specs=[SMEM, VMEM, ANY],
-        out_specs=[VMEM, ANY],
-        out_shape=[shape((2, 16, 40, 128), f32), shape((cells, cols), bf16)],
-        scratch_shapes=[
-            pltpu.VMEM((cells, cols), bf16),
             pltpu.VMEM((cells, 4, cols // 4), f32),
             pltpu.VMEM((cells, 4, cols // 4), f32),
+            pltpu.VMEM((2, 16, 40, 128), f32),
             pltpu.VMEM((16, 40, 128), f32),
             pltpu.VMEM((16, 40, 128), f32),
             pltpu.VMEM((16, 40, 128), f32),
             pltpu.VMEM((8, 40, 128), f32),
             pltpu.VMEM((2, 40, 128), f32),
             pltpu.VMEM((16, 40, 128), f32),
-            *[dma((n,)) for n in (1, 1, 15, 15, 7, 7, 15, 15, 1, 1)],
+            dma((2,)),
             dma(()),
-            dma((4,)),
+            dma((4, 4)),
+            dma((4, 4)),
+            *[dma((2,) + n) for n in ((), (), (15,), (15,), (7,), (7,), (15,), (15,), (), ())],
         ],
         compiler_params=pltpu.CompilerParams(
-            collective_id=1, has_side_effects=True, vmem_limit_bytes=BIG
+            collective_id=0, has_side_effects=True, vmem_limit_bytes=BIG
         ),
-    )(wet_index, gram.reshape(2, 16, 40, 128), f)
+    )(
+        wet_index,
+        wet_index.reshape(nx, ny),
+        wet_count,
+        lon_metric,
+        lat_metric,
+        velocity.reshape(cols, nx, ny),
+    )
 
     scale = math.sqrt(cells * n_lat * n_lon)
     basis, r_factor = pl.pallas_call(

time: 88.9 us -> 84.2 us (0.947)
  Pallas kernels: 87.2 us -> 82.5 us
    pallas_call x2 -> x1, Pallas kernels: 58.5 us -> 53.8 us  [shards(): pl.pallas_call(functools.partial(field_kernel, n_lat, n_lon), in_specs=[S...]
where the time goes in v4:
time: 84.2 us; the launch traced here: 84 us
  Pallas kernels  82.5 us (98%)
  between operations  1.47 us (2%)
    pallas_call x1, Pallas kernels, shards(): pl.pallas_call(functools.partial(field_kernel, n_lat, n_lon), in_specs=[S...  53.8 us
    pallas_call x1, Pallas kernels, shards(): pl.pallas_call(functools.partial(factor_kernel, scale), in_specs=[VMEM, A...  28.7 us

profile of v4, /device:TPU:1, one launch (start us, length us, event | category | flops | bytes accessed | tf_op | source)
XLA Modules:
  0.0 84.0 jit_solution(9037230082262241682)
XLA Ops:
  1.3 53.8 %shard_map.68 = (f32[2,16,40,128]{3,2,1,0:T(8,128)}, bf16[6144,512]{1,0:T(8,128)(2,1)}) custom-call(s32[6144]{0:T(1024)} %order.1, s32[48,128]{1,0:T(8,128)} %bitcast.5, s32[1]{0:T(128)S(6)} %copy.7.count, f32[48,128]{1,0:T(8,128)} %lon_ref.1, f32[48,128]{1,0:T(8,128)} %lat_ref.1, bf16[512,48,128]{2,1,0:T(8,128)(2,1)} %bitcast.3), custom_call_target="tpu_custom_call" | custom-call | tf_op jit(solution)/shard_map/pallas_call | solution.py:546
  55.1 28.7 %shard_map.69 = (bf16[512,6144]{1,0:T(8,128)(2,1)}, f32[512,512]{1,0:T(8,128)}) custom-call(f32[10,128,128]{2,1,0:T(8,128)} %bitcast.4, bf16[6144,512]{1,0:T(8,128)(2,1)} %get-tuple-element.5.t_hbm), custom_call_target="tpu_custom_call" | custom-call | tf_op jit(solution)/shard_map/pallas_call | solution.py:592

commit v5 on v4

--- a/solution.py
+++ b/solution.py
@@ -178,33 +178,52 @@
         cu, cv = h, 2 + h
         lu, lv = slice(cu * lane, cu * lane + lane), slice(cv * lane, cv * lane + lane)
 
-        def fields(at_group, _):
+        def fields(at_group, at, m_lon, m_lat):
+            x = at_group * group + at
+            x_top = x + top * (nx - 1 - 2 * x)
+            here = pl.ds(x * ny if h else pl.multiple_of(x * ny, ny), ny)
+            a, b = m_lon[:, at : at + 1], m_lat[:, at : at + 1]
+            u_x = vt[x + 2, :, lu].astype(jnp.float32) - vt[x, :, lu].astype(jnp.float32)
+            v_x = vt[x + 2, :, lv].astype(jnp.float32) - vt[x, :, lv].astype(jnp.float32)
+
+            def over_y(c, where):
+                inner = lax.dot_general(
+                    band, vt[x + 1, :, where], NN, preferred_element_type=jnp.float32
+                )
+                inner = inner + jnp.where(row == ny - 1, north[c, pl.ds(x_top, 1), :], 0.0)
+                return inner - jnp.where(row == 0, south[c, pl.ds(x, 1), :], 0.0)
+
+            f[here, lu] = (a * v_x - b * over_y(cu, lu)).astype(jnp.bfloat16)
+            f[here, lv] = (a * u_x + b * over_y(cv, lv)).astype(jnp.bfloat16)
+
+        def multiply(at_group, low, high):
+            span = pl.ds(at_group * group * ny, group * ny)
+            acc[low:high, low:] += lax.dot_general(
+                f[span, low:high], f[span, low:], TN, preferred_element_type=jnp.float32
+            )
+
+        def fields_of_group(at_group, _):
             m_lon, m_lat = lon_t[at_group], lat_t[at_group]
             for at in range(group):
-                x = at_group * group + at
-                x_top = x + top * (nx - 1 - 2 * x)
-                here = pl.ds(pl.multiple_of(x * ny, ny), ny)
-                a, b = m_lon[:, at : at + 1], m_lat[:, at : at + 1]
-                u_x = vt[x + 2, :, lu].astype(jnp.float32) - vt[x, :, lu].astype(jnp.float32)
-                v_x = vt[x + 2, :, lv].astype(jnp.float32) - vt[x, :, lv].astype(jnp.float32)
-
-                def over_y(c, where):
-                    inner = lax.dot_general(
-                        band, vt[x + 1, :, where], NN, preferred_element_type=jnp.float32
-                    )
-                    inner = inner + jnp.where(row == ny - 1, north[c, pl.ds(x_top, 1), :], 0.0)
-                    return inner - jnp.where(row == 0, south[c, pl.ds(x, 1), :], 0.0)
-
-                f[here, lu] = (a * v_x - b * over_y(cu, lu)).astype(jnp.bfloat16)
-                f[here, lv] = (a * u_x + b * over_y(cv, lv)).astype(jnp.bfloat16)
-            if h == 1:
-                span = pl.ds(pl.multiple_of(at_group * (group * ny), group * ny), group * ny)
-                acc[...] += lax.dot_general(
-                    f[span, :], f[span, :], TN, preferred_element_type=jnp.float32
-                )
+                fields(at_group, at, m_lon, m_lat)
             return 0
 
-        lax.fori_loop(0, nx // group, fields, 0)
+        groups = nx // group
+        middle = acc.shape[0] // 2
+        if h == 0:
+            lax.fori_loop(0, groups, fields_of_group, 0)
+        else:
+            for at_group in range(groups):
+                m_lon, m_lat = lon_t[at_group], lat_t[at_group]
+                for at in range(group):
+                    fields(at_group, at, m_lon, m_lat)
+                    if at_group and at == 3:
+                        multiply(at_group - 1, 0, middle)
+                    if at_group and at == 11:
+                        multiply(at_group - 1, middle, 2 * middle)
+            multiply(groups - 1, 0, middle)
+            multiply(groups - 1, middle, 2 * middle)
+
     tile = 0
     for i in range(4):
         for j in range(i, 4):

time: 84.2 us -> 82.8 us (0.983)
  Pallas kernels: 82.5 us -> 81 us
    pallas_call x1, Pallas kernels: 53.8 us -> 52.3 us  [shards(): pl.pallas_call(functools.partial(field_kernel, n_lat, n_lon), in_specs=[S...]
where the time goes in v5:
time: 82.8 us; the launch traced here: 82.5 us
  Pallas kernels  81 us (98%)
  between operations  1.47 us (2%)
    pallas_call x1, Pallas kernels, shards(): pl.pallas_call(functools.partial(field_kernel, n_lat, n_lon), in_specs=[S...  52.3 us
    pallas_call x1, Pallas kernels, shards(): pl.pallas_call(functools.partial(factor_kernel, scale), in_specs=[VMEM, A...  28.7 us

profile of v5, /device:TPU:1, one launch (start us, length us, event | category | flops | bytes accessed | tf_op | source)
XLA Modules:
  0.0 82.5 jit_solution(15537409878657992531)
XLA Ops:
  1.3 52.3 %shard_map.68 = (f32[2,16,40,128]{3,2,1,0:T(8,128)}, bf16[6144,512]{1,0:T(8,128)(2,1)}) custom-call(s32[6144]{0:T(1024)} %order.1, s32[48,128]{1,0:T(8,128)} %bitcast.5, s32[1]{0:T(128)S(6)} %copy.7.count, f32[48,128]{1,0:T(8,128)} %lon_ref.1, f32[48,128]{1,0:T(8,128)} %lat_ref.1, bf16[512,48,128]{2,1,0:T(8,128)(2,1)} %bitcast.3), custom_call_target="tpu_custom_call" | custom-call | tf_op jit(solution)/shard_map/pallas_call | solution.py:565
  53.6 28.7 %shard_map.69 = (bf16[512,6144]{1,0:T(8,128)(2,1)}, f32[512,512]{1,0:T(8,128)}) custom-call(f32[10,128,128]{2,1,0:T(8,128)} %bitcast.4, bf16[6144,512]{1,0:T(8,128)(2,1)} %get-tuple-element.5.t_hbm), custom_call_target="tpu_custom_call" | custom-call | tf_op jit(solution)/shard_map/pallas_call | solution.py:611

commit v6 on v5

--- a/solution.py
+++ b/solution.py
@@ -234,7 +234,7 @@
                 ]
                 tile += 1
     cells, cols = f.shape
-    spans = (pl.ds(0, 24), pl.ds(24, 16))
+    spans = (pl.ds(0, 16), pl.ds(16, 16), pl.ds(32, 8))
     started = []
 
     def widen(at, _):
@@ -339,22 +339,25 @@
             item.wait_recv()
         return go(r3.at[:, span], out.at[core, :, span], send4.at[k], recv4.at[k], mate)
 
-    pairs = [pair_start(k) for k in range(2)]
+    parts = range(len(spans))
+    pairs = [pair_start(k) for k in parts]
     lax.fori_loop(0, cells // 128, widen, 0)
-    planes = [gather_start(k, pairs[k]) for k in range(2)]
-    pick_part(0, 4)
-    first = column_start(0, planes[0])
-    pick_part(4, 5)
-    columns = [first, column_start(1, planes[1])]
-    pick_part(5, 8)
-    first = back_start(0, columns[0])
-    pick_part(8, 9)
-    backs = [first, back_start(1, columns[1])]
-    pick_part(9, 12)
+    planes = [gather_start(k, pairs[k]) for k in parts]
+    pick_part(0, 3)
+    columns = []
+    for k in parts:
+        columns.append(column_start(k, planes[k]))
+        pick_part(3 + k, 4 + k)
+    pick_part(6, 7)
+    backs = []
+    for k in parts:
+        backs.append(back_start(k, columns[k]))
+        pick_part(7 + k, 8 + k)
+    pick_part(10, 12)
     lax.fori_loop(0, cells // 128, narrow, 0)
     store = pltpu.make_async_copy(f, t_hbm, store_sem)
     store.start()
-    lasts = [last_start(k, backs[k]) for k in range(2)]
+    lasts = [last_start(k, backs[k]) for k in parts]
     out[core] = r3[...]
     for item in lasts:
         item.wait_recv()
@@ -593,7 +596,7 @@
             dma(()),
             dma((4, 4)),
             dma((4, 4)),
-            *[dma((2,) + n) for n in ((), (), (15,), (15,), (7,), (7,), (15,), (15,), (), ())],
+            *[dma((3,) + n) for n in ((), (), (15,), (15,), (7,), (7,), (15,), (15,), (), ())],
         ],
         compiler_params=pltpu.CompilerParams(
             collective_id=0, has_side_effects=True, vmem_limit_bytes=BIG

time: 82.8 us -> 82.8 us (level)
  no operation moved by 1% of the time
where the time goes in v6:
time: 82.8 us; the launch traced here: 82.5 us
  Pallas kernels  81.1 us (98%)
  between operations  1.47 us (2%)
    pallas_call x1, Pallas kernels, shards(): pl.pallas_call(functools.partial(field_kernel, n_lat, n_lon), in_specs=[S...  52.4 us
    pallas_call x1, Pallas kernels, shards(): pl.pallas_call(functools.partial(factor_kernel, scale), in_specs=[VMEM, A...  28.7 us

profile of v6, /device:TPU:1, one launch (start us, length us, event | category | flops | bytes accessed | tf_op | source)
XLA Modules:
  0.0 82.5 jit_solution(3696947198342738718)
XLA Ops:
  1.3 52.4 %shard_map.68 = (f32[2,16,40,128]{3,2,1,0:T(8,128)}, bf16[6144,512]{1,0:T(8,128)(2,1)}) custom-call(s32[6144]{0:T(1024)} %order.1, s32[48,128]{1,0:T(8,128)} %bitcast.5, s32[1]{0:T(128)S(6)} %copy.7.count, f32[48,128]{1,0:T(8,128)} %lon_ref.1, f32[48,128]{1,0:T(8,128)} %lat_ref.1, bf16[512,48,128]{2,1,0:T(8,128)(2,1)} %bitcast.3), custom_call_target="tpu_custom_call" | custom-call | tf_op jit(solution)/shard_map/pallas_call | solution.py:568
  53.7 28.7 %shard_map.69 = (bf16[512,6144]{1,0:T(8,128)(2,1)}, f32[512,512]{1,0:T(8,128)}) custom-call(f32[10,128,128]{2,1,0:T(8,128)} %bitcast.4, bf16[6144,512]{1,0:T(8,128)(2,1)} %get-tuple-element.5.t_hbm), custom_call_target="tpu_custom_call" | custom-call | tf_op jit(solution)/shard_map/pallas_call | solution.py:614
